TPU v7x, 32 devices: a whole 2x2x4 slice. The times are simulated.
32 devices in a mesh: gx: 4 (over y, x), gy: 4 (over z), gz: 2 (over core).
Axes of the slice: x: 2, y: 2, z: 4, core: 2. Of those that a mesh axis runs over, the one named last changes fastest.
Arguments:
- state: float32 [3, 32, 160, 512], P(None, 'gz', 'gy', 'gx'), may hold values from -6 to 6
- right_side: float32 [3, 32, 160, 512], P(None, 'gz', 'gy', 'gx'), may hold values from -6 to 6
- permeability: bfloat16 [32, 160, 512], P('gz', 'gy', 'gx'), may hold values from 0.099609375 to 10
- pore_volume: bfloat16 [32, 160, 512], P('gz', 'gy', 'gx'), may hold values from 0.019897461 to 0.19921875
- facies: int32 [32], P('gz'), may hold values from 0 to 3
- storage_table: float32 [4, 3, 3], replicated, may hold values from -0.3 to 2, as said below
- coupling_table: float32 [4, 3, 3], replicated, may hold values from -0.3 to 2, as said below
Outputs:
- new_state: float32 [3, 32, 160, 512], P(None, 'gz', 'gy', 'gx')
- correction: float32 [160, 512], P('gy', 'gx')
Inputs may be any that keep to these rules, and one draw needn't show every extreme that they name: `storage_table`: each facies block has a diagonal of 1 to 2 and off-diagonal entries of magnitude at most 0.3. `coupling_table`: each facies block has a diagonal of 1 to 2 and off-diagonal entries of magnitude at most 0.3.
All inputs are finite; a program needn't handle non-finite values.
Results may differ from a plain program's by a relative error of at most 0.0003.
Values sent between devices are 32-bit elements; how exact they have to be, the bound alone decides.
A program may use at most 64 MiB of HBM per device.

v0:
```python
import jax
import jax.numpy as jnp
from jax import lax
from jax.sharding import PartitionSpec as P

SWEEPS = 8


relax = 0.8


def extended(cells, sides, width):
    for axis, dim in sides:
        count = lax.axis_size(axis)
        ends = count - 1
        head = lax.slice_in_dim(cells, 0, width, axis=dim)
        tail = lax.slice_in_dim(cells, cells.shape[dim] - width, cells.shape[dim], axis=dim)
        cells = jnp.concatenate(
            [
                lax.ppermute(tail, axis, [(i, (i + 1) % count) for i in range(ends)]),
                cells,
                lax.ppermute(head, axis, [((i + 1) % count, i) for i in range(ends)]),
            ],
            axis=dim,
        )
    return cells


def layer_tables(facies, table):
    onehot = (facies[:, None] == jnp.arange(table.shape[0])[None, :]).astype(jnp.float32)
    return jnp.dot(onehot, table.reshape(table.shape[0], 9), precision=lax.Precision.HIGHEST)


def layer_coefficient(rows, row_index, column_index):
    return rows[:, 3 * row_index + column_index][:, None, None]


def neighbours(padded):
    return [
        padded[..., 2:, 1:-1, 1:-1],
        padded[..., :-2, 1:-1, 1:-1],
        padded[..., 1:-1, 2:, 1:-1],
        padded[..., 1:-1, :-2, 1:-1],
        padded[..., 1:-1, 1:-1, 2:],
        padded[..., 1:-1, 1:-1, :-2],
    ]


def face_weights(padded_perm):
    center = padded_perm[1:-1, 1:-1, 1:-1]
    return [2.0 * center * nearby / (center + nearby) for nearby in neighbours(padded_perm)]


def apply_operator(padded_state, weights, storage, storage_rows, coupling_rows):
    center = padded_state[:, 1:-1, 1:-1, 1:-1]
    fluxes = jnp.zeros_like(center)
    for weight, nearby in zip(weights, neighbours(padded_state)):
        fluxes = fluxes + weight[None] * (center - nearby)
    outputs = []
    for row_index in range(3):
        local = sum((layer_coefficient(storage_rows, row_index, k) * center[k] for k in range(3)))
        moved = sum((layer_coefficient(coupling_rows, row_index, k) * fluxes[k] for k in range(3)))
        outputs.append(storage * local + moved)
    return jnp.stack(outputs)


def coarse_planes(residual, weights, storage, storage_rows, coupling_rows):
    first_coupling = layer_coefficient(coupling_rows, 0, 0)
    first_storage = layer_coefficient(storage_rows, 0, 0)
    items = [residual[0], storage * first_storage] + [
        weights[k] * first_coupling for k in range(2, 6)
    ]
    return jnp.stack([jnp.sum(item, axis=0) for item in items])


def jacobi(field, bordered, planes):
    diagonal = planes[1] + planes[2] + planes[3] + planes[4] + planes[5]
    nearby = (
        planes[2] * bordered[2:, 1:-1]
        + planes[3] * bordered[:-2, 1:-1]
        + planes[4] * bordered[1:-1, 2:]
        + planes[5] * bordered[1:-1, :-2]
    )
    return field + relax * (planes[0] - diagonal * field + nearby) / diagonal


def column_image(correction, bordered, weights, storage, storage_rows, coupling_rows):
    areal = (
        weights[2] * (correction - bordered[2:, 1:-1])
        + weights[3] * (correction - bordered[:-2, 1:-1])
        + weights[4] * (correction - bordered[1:-1, 2:])
        + weights[5] * (correction - bordered[1:-1, :-2])
    )
    return jnp.stack(
        [
            storage * layer_coefficient(storage_rows, r, 0) * correction
            + layer_coefficient(coupling_rows, r, 0) * areal
            for r in range(3)
        ]
    )


def block_solve(weights, storage, storage_rows, coupling_rows, residual):
    face_total = weights[0] + weights[1] + weights[2] + weights[3] + weights[4] + weights[5]
    entries = [
        [
            storage * layer_coefficient(storage_rows, r, c)
            + face_total * layer_coefficient(coupling_rows, r, c)
            for c in range(3)
        ]
        for r in range(3)
    ]

    def cofactor(r, c):
        return (
            entries[(r + 1) % 3][(c + 1) % 3] * entries[(r + 2) % 3][(c + 2) % 3]
            - entries[(r + 1) % 3][(c + 2) % 3] * entries[(r + 2) % 3][(c + 1) % 3]
        )

    factors = [[cofactor(r, c) for c in range(3)] for r in range(3)]
    determinant = (
        entries[0][0] * factors[0][0]
        + entries[0][1] * factors[0][1]
        + entries[0][2] * factors[0][2]
    )
    return jnp.stack(
        [
            (
                factors[0][r] * residual[0]
                + factors[1][r] * residual[1]
                + factors[2][r] * residual[2]
            )
            / determinant
            for r in range(3)
        ]
    )


def per_device(state, right_side, permeability, pore_volume, facies, storage_table, coupling_table):
    perm_wide = permeability.astype(jnp.float32)
    storage = pore_volume.astype(jnp.float32)
    storage_rows = layer_tables(facies, storage_table)
    coupling_rows = layer_tables(facies, coupling_table)
    stacked = jnp.concatenate([state, perm_wide[None]], axis=0)
    padded = extended(stacked, (("gz", 1), ("gy", 2), ("gx", 3)), 1)
    weights = face_weights(padded[3])
    residual = right_side - apply_operator(
        padded[:3], weights, storage, storage_rows, coupling_rows
    )
    planes = coarse_planes(residual, weights, storage, storage_rows, coupling_rows)
    totals = lax.psum(planes, "gz")
    correction = jnp.zeros(totals.shape[1:], jnp.float32)
    for repeat_index in range(SWEEPS):
        bordered = extended(correction, (("gy", 0), ("gx", 1)), 1)
        correction = jacobi(correction, bordered, totals)
    state_one = state.at[0].add(correction[None])
    bordered = extended(correction, (("gy", 0), ("gx", 1)), 1)
    later_residual = residual - column_image(
        correction, bordered, weights, storage, storage_rows, coupling_rows
    )
    new_state = state_one + block_solve(
        weights, storage, storage_rows, coupling_rows, later_residual
    )
    return (new_state, correction)


def solution(mesh):
    return jax.shard_map(
        per_device,
        mesh=mesh,
        in_specs=(
            P(None, "gz", "gy", "gx"),
            P(None, "gz", "gy", "gx"),
            P("gz", "gy", "gx"),
            P("gz", "gy", "gx"),
            P("gz"),
            P(),
            P(),
        ),
        out_specs=(P(None, "gz", "gy", "gx"), P("gy", "gx")),
        check_vma=False,
    )
```

profile of v0, /device:TPU:28, one launch (start us, length us, event | category | flops | bytes accessed | tf_op | source)
XLA Modules:
  0.0 220.8 jit_solution(13019892907075081389)
XLA Ops:
  8.5 2.3 %collective-permute-start.6 = (f32[1,128]{1,0:T(1,128)S(1)}, f32[1,128]{1,0:T(1,128)S(1)}, u32[]{:S(2)}, u32[]{:S(2)}) collective-permute-start(f32[1,128]{1,0:T(1,128)S(1)} %broadcast.60), channel_id=1, source_target_pairs={{2,0},{4,2},{6,4},{3,1},{5,3},{7,5},{10,8},{12,10},{14,12},{11,9},... | collective-permute-start | bytes 1544 | tf_op jit(solution)/shard_map/ppermute | solution.py:22
  18.2 5.0 %collective-permute-start.3 = (f32[4,18,1,128]{3,0,2,1:T(4,128)S(1)}, f32[4,18,1,128]{3,0,2,1:T(4,128)S(1)}, u32[]{:S(2)}, u32[]{:S(2)}) collective-permute-start(f32[4,18,1,128]{3,0,2,1:T(4,128)S(1)} %copy.245), channel_id=1, source_target_pairs={{2,0},{4,2},{6,4},{3,1},{5,3},{7,5},{10,8},{12,10},{14,12},{11,9},... | collective-permute-start | bytes 110600 | tf_op jit(solution)/shard_map/ppermute | solution.py:22
  26.9 2.2 copy.218
  29.1 3.4 %collective-permute-start.4 = (f32[4,18,42,1]{2,0,3,1:T(4,128)S(1)}, f32[4,18,42,1]{2,0,3,1:T(4,128)S(1)}, u32[]{:S(2)}, u32[]{:S(2)}) collective-permute-start(f32[4,18,42,1]{2,0,3,1:T(4,128)S(1)} %copy.218), channel_id=1, source_target_pairs={{0,8},{8,16},{16,24},{1,9},{9,17},{17,25},{2,10},{10,18},{18,26},{... | collective-permute-start | bytes 36296 | tf_op jit(solution)/shard_map/ppermute | solution.py:20
  33.2 3.3 %collective-permute-start.5 = (f32[4,18,42,1]{2,0,3,1:T(4,128)S(1)}, f32[4,18,42,1]{2,0,3,1:T(4,128)S(1)}, u32[]{:S(2)}, u32[]{:S(2)}) collective-permute-start(f32[4,18,42,1]{2,0,3,1:T(4,128)S(1)} %copy.219), channel_id=1, source_target_pairs={{8,0},{16,8},{24,16},{9,1},{17,9},{25,17},{10,2},{18,10},{26,18},{... | collective-permute-start | bytes 36296 | tf_op jit(solution)/shard_map/ppermute | solution.py:22
  44.0 3.3 %fusion.2 = f32[3,16,40,128]{3,2,1,0:T(8,128)S(1)} fusion(f32[3,16,40,128]{3,2,1,0:T(8,128)S(1)} %copy.254, f32[4,18,42,1]{3,2,1,0:T(8,128)S(1)} %copy.220, f32[4,18,1,128]{3,2,1,0:T(1,128)S(1)} %copy.217, f32[4,18,1,128]{3,2,1,0:T(1,128)S(1)} %copy.216, f32[4,1,40,128]{3,2,1,0:T(8,128)S(1)} %collective-permute-done.1, ...), kind=kLoop, calls=%fused_computation.18 | loop fusion | flops 10076160 | bytes 4521600 | tf_op jit(solution)/shard_map/add | solution.py:58
  51.7 4.2 %collective-permute-start.8 = (f32[42,1]{1,0:T(8,128)S(1)}, f32[42,1]{1,0:T(8,128)S(1)}, u32[]{:S(2)}, u32[]{:S(2)}) collective-permute-start(f32[42,1]{1,0:T(8,128)S(1)} %get-tuple-element.66), channel_id=1, source_target_pairs={{8,0},{16,8},{24,16},{9,1},{17,9},{25,17},{10,2},{18,10},{26,18},{... | collective-permute-start | bytes 512 | tf_op jit(solution)/shard_map/ppermute | solution.py:22
  56.0 1.9 collective-permute-start.9
  57.9 4.7 %collective-permute-done.9 = f32[42,1]{1,0:T(8,128)S(1)} collective-permute-done((f32[42,1]{1,0:T(8,128)S(1)}, f32[42,1]{1,0:T(8,128)S(1)}, u32[]{:S(2)}, u32[]{:S(2)}) %collective-permute-start.9) | collective-permute-done | bytes 200 | tf_op jit(solution)/shard_map/ppermute | solution.py:20
  62.6 9.7 %all-reduce.4.cloned.1.call-done = f32[6,40,128]{2,1,0:T(8,128)} async-done(((f32[6,40,128]{2,1,0:T(8,128)}), f32[6,40,128]{2,1,0:T(8,128)}) %all-reduce.4.cloned.1.call-update) | async-done | bytes 122896 | tf_op jit(solution)/shard_map/psum | solution.py:151
  73.3 2.4 %collective-permute-start.10 = (f32[1,128]{1,0:T(1,128)S(1)}, f32[1,128]{1,0:T(1,128)S(1)}, u32[]{:S(2)}, u32[]{:S(2)}) collective-permute-start(f32[1,128]{1,0:T(1,128)S(1)} %get-tuple-element.87), channel_id=1, source_target_pairs={{2,0},{4,2},{6,4},{3,1},{5,3},{7,5},{10,8},{12,10},{14,12},{11,9},... | collective-permute-start | bytes 1544 | tf_op jit(solution)/shard_map/ppermute | solution.py:22
  77.2 4.2 %collective-permute-done.11 = f32[1,128]{1,0:T(1,128)S(1)} collective-permute-done((f32[1,128]{1,0:T(1,128)S(1)}, f32[1,128]{1,0:T(1,128)S(1)}, u32[]{:S(2)}, u32[]{:S(2)}) %collective-permute-start.11) | collective-permute-done | bytes 544 | tf_op jit(solution)/shard_map/ppermute | solution.py:20
  81.4 3.4 %collective-permute-start.12 = (f32[42,1]{1,0:T(8,128)S(1)}, f32[42,1]{1,0:T(8,128)S(1)}, u32[]{:S(2)}, u32[]{:S(2)}) collective-permute-start(f32[42,1]{1,0:T(8,128)S(1)} %get-tuple-element.64), channel_id=1, source_target_pairs={{8,0},{16,8},{24,16},{9,1},{17,9},{25,17},{10,2},{18,10},{26,18},{... | collective-permute-start | bytes 512 | tf_op jit(solution)/shard_map/ppermute | solution.py:22
  84.8 2.5 %collective-permute-start.13 = (f32[42,1]{1,0:T(8,128)S(1)}, f32[42,1]{1,0:T(8,128)S(1)}, u32[]{:S(2)}, u32[]{:S(2)}) collective-permute-start(f32[42,1]{1,0:T(8,128)S(1)} %get-tuple-element.65), channel_id=1, source_target_pairs={{0,8},{8,16},{16,24},{1,9},{9,17},{17,25},{2,10},{10,18},{18,26},{... | collective-permute-start | bytes 512 | tf_op jit(solution)/shard_map/ppermute | solution.py:20
  87.3 4.1 %collective-permute-done.13 = f32[42,1]{1,0:T(8,128)S(1)} collective-permute-done((f32[42,1]{1,0:T(8,128)S(1)}, f32[42,1]{1,0:T(8,128)S(1)}, u32[]{:S(2)}, u32[]{:S(2)}) %collective-permute-start.13) | collective-permute-done | bytes 200 | tf_op jit(solution)/shard_map/ppermute | solution.py:20
  92.3 2.4 %collective-permute-start.14 = (f32[1,128]{1,0:T(1,128)S(1)}, f32[1,128]{1,0:T(1,128)S(1)}, u32[]{:S(2)}, u32[]{:S(2)}) collective-permute-start(f32[1,128]{1,0:T(1,128)S(1)} %get-tuple-element.85), channel_id=1, source_target_pairs={{2,0},{4,2},{6,4},{3,1},{5,3},{7,5},{10,8},{12,10},{14,12},{11,9},... | collective-permute-start | bytes 1544 | tf_op jit(solution)/shard_map/ppermute | solution.py:22
  96.1 4.2 %collective-permute-done.15 = f32[1,128]{1,0:T(1,128)S(1)} collective-permute-done((f32[1,128]{1,0:T(1,128)S(1)}, f32[1,128]{1,0:T(1,128)S(1)}, u32[]{:S(2)}, u32[]{:S(2)}) %collective-permute-start.15) | collective-permute-done | bytes 544 | tf_op jit(solution)/shard_map/ppermute | solution.py:20
  100.4 1.9 collective-permute-start.16
  102.3 3.9 %collective-permute-start.17 = (f32[42,1]{1,0:T(8,128)S(1)}, f32[42,1]{1,0:T(8,128)S(1)}, u32[]{:S(2)}, u32[]{:S(2)}) collective-permute-start(f32[42,1]{1,0:T(8,128)S(1)} %get-tuple-element.63), channel_id=1, source_target_pairs={{0,8},{8,16},{16,24},{1,9},{9,17},{17,25},{2,10},{10,18},{18,26},{... | collective-permute-start | bytes 512 | tf_op jit(solution)/shard_map/ppermute | solution.py:20
  106.2 2.7 %collective-permute-done.17 = f32[42,1]{1,0:T(8,128)S(1)} collective-permute-done((f32[42,1]{1,0:T(8,128)S(1)}, f32[42,1]{1,0:T(8,128)S(1)}, u32[]{:S(2)}, u32[]{:S(2)}) %collective-permute-start.17) | collective-permute-done | bytes 200 | tf_op jit(solution)/shard_map/ppermute | solution.py:20
  109.8 2.4 %collective-permute-start.18 = (f32[1,128]{1,0:T(1,128)S(1)}, f32[1,128]{1,0:T(1,128)S(1)}, u32[]{:S(2)}, u32[]{:S(2)}) collective-permute-start(f32[1,128]{1,0:T(1,128)S(1)} %get-tuple-element.83), channel_id=1, source_target_pairs={{2,0},{4,2},{6,4},{3,1},{5,3},{7,5},{10,8},{12,10},{14,12},{11,9},... | collective-permute-start | bytes 1544 | tf_op jit(solution)/shard_map/ppermute | solution.py:22
  113.6 4.2 %collective-permute-done.19 = f32[1,128]{1,0:T(1,128)S(1)} collective-permute-done((f32[1,128]{1,0:T(1,128)S(1)}, f32[1,128]{1,0:T(1,128)S(1)}, u32[]{:S(2)}, u32[]{:S(2)}) %collective-permute-start.19) | collective-permute-done | bytes 544 | tf_op jit(solution)/shard_map/ppermute | solution.py:20
  117.8 1.9 collective-permute-start.20
  119.7 3.9 %collective-permute-start.21 = (f32[42,1]{1,0:T(8,128)S(1)}, f32[42,1]{1,0:T(8,128)S(1)}, u32[]{:S(2)}, u32[]{:S(2)}) collective-permute-start(f32[42,1]{1,0:T(8,128)S(1)} %get-tuple-element.61), channel_id=1, source_target_pairs={{0,8},{8,16},{16,24},{1,9},{9,17},{17,25},{2,10},{10,18},{18,26},{... | collective-permute-start | bytes 512 | tf_op jit(solution)/shard_map/ppermute | solution.py:20
  123.7 2.7 %collective-permute-done.21 = f32[42,1]{1,0:T(8,128)S(1)} collective-permute-done((f32[42,1]{1,0:T(8,128)S(1)}, f32[42,1]{1,0:T(8,128)S(1)}, u32[]{:S(2)}, u32[]{:S(2)}) %collective-permute-start.21) | collective-permute-done | bytes 200 | tf_op jit(solution)/shard_map/ppermute | solution.py:20
  127.3 1.9 collective-permute-start.22
  130.5 4.2 %collective-permute-done.23 = f32[1,128]{1,0:T(1,128)S(1)} collective-permute-done((f32[1,128]{1,0:T(1,128)S(1)}, f32[1,128]{1,0:T(1,128)S(1)}, u32[]{:S(2)}, u32[]{:S(2)}) %collective-permute-start.23) | collective-permute-done | bytes 544 | tf_op jit(solution)/shard_map/ppermute | solution.py:20
  134.8 1.9 collective-permute-start.24
  136.7 3.9 %collective-permute-start.25 = (f32[42,1]{1,0:T(8,128)S(1)}, f32[42,1]{1,0:T(8,128)S(1)}, u32[]{:S(2)}, u32[]{:S(2)}) collective-permute-start(f32[42,1]{1,0:T(8,128)S(1)} %get-tuple-element.59), channel_id=1, source_target_pairs={{0,8},{8,16},{16,24},{1,9},{9,17},{17,25},{2,10},{10,18},{18,26},{... | collective-permute-start | bytes 512 | tf_op jit(solution)/shard_map/ppermute | solution.py:20
  140.6 2.7 %collective-permute-done.25 = f32[42,1]{1,0:T(8,128)S(1)} collective-permute-done((f32[42,1]{1,0:T(8,128)S(1)}, f32[42,1]{1,0:T(8,128)S(1)}, u32[]{:S(2)}, u32[]{:S(2)}) %collective-permute-start.25) | collective-permute-done | bytes 200 | tf_op jit(solution)/shard_map/ppermute | solution.py:20
  144.2 1.9 collective-permute-start.26
  147.5 4.2 %collective-permute-done.27 = f32[1,128]{1,0:T(1,128)S(1)} collective-permute-done((f32[1,128]{1,0:T(1,128)S(1)}, f32[1,128]{1,0:T(1,128)S(1)}, u32[]{:S(2)}, u32[]{:S(2)}) %collective-permute-start.27) | collective-permute-done | bytes 544 | tf_op jit(solution)/shard_map/ppermute | solution.py:20
  151.7 1.9 collective-permute-start.28
  153.6 3.9 %collective-permute-start.29 = (f32[42,1]{1,0:T(8,128)S(1)}, f32[42,1]{1,0:T(8,128)S(1)}, u32[]{:S(2)}, u32[]{:S(2)}) collective-permute-start(f32[42,1]{1,0:T(8,128)S(1)} %get-tuple-element.57), channel_id=1, source_target_pairs={{0,8},{8,16},{16,24},{1,9},{9,17},{17,25},{2,10},{10,18},{18,26},{... | collective-permute-start | bytes 512 | tf_op jit(solution)/shard_map/ppermute | solution.py:20
  157.6 2.7 %collective-permute-done.29 = f32[42,1]{1,0:T(8,128)S(1)} collective-permute-done((f32[42,1]{1,0:T(8,128)S(1)}, f32[42,1]{1,0:T(8,128)S(1)}, u32[]{:S(2)}, u32[]{:S(2)}) %collective-permute-start.29) | collective-permute-done | bytes 200 | tf_op jit(solution)/shard_map/ppermute | solution.py:20
  160.4 1.9 collective-permute-start.30
  163.6 4.2 %collective-permute-done.31 = f32[1,128]{1,0:T(1,128)S(1)} collective-permute-done((f32[1,128]{1,0:T(1,128)S(1)}, f32[1,128]{1,0:T(1,128)S(1)}, u32[]{:S(2)}, u32[]{:S(2)}) %collective-permute-start.31) | collective-permute-done | bytes 544 | tf_op jit(solution)/shard_map/ppermute | solution.py:20
  167.8 1.9 collective-permute-start.32
  169.7 3.9 %collective-permute-start.33 = (f32[42,1]{1,0:T(8,128)S(1)}, f32[42,1]{1,0:T(8,128)S(1)}, u32[]{:S(2)}, u32[]{:S(2)}) collective-permute-start(f32[42,1]{1,0:T(8,128)S(1)} %get-tuple-element.55), channel_id=1, source_target_pairs={{0,8},{8,16},{16,24},{1,9},{9,17},{17,25},{2,10},{10,18},{18,26},{... | collective-permute-start | bytes 512 | tf_op jit(solution)/shard_map/ppermute | solution.py:20
  173.7 2.7 %collective-permute-done.33 = f32[42,1]{1,0:T(8,128)S(1)} collective-permute-done((f32[42,1]{1,0:T(8,128)S(1)}, f32[42,1]{1,0:T(8,128)S(1)}, u32[]{:S(2)}, u32[]{:S(2)}) %collective-permute-start.33) | collective-permute-done | bytes 200 | tf_op jit(solution)/shard_map/ppermute | solution.py:20
  176.5 2.0 collective-permute-start.34
  179.9 4.2 %collective-permute-done.35 = f32[1,128]{1,0:T(1,128)S(1)} collective-permute-done((f32[1,128]{1,0:T(1,128)S(1)}, f32[1,128]{1,0:T(1,128)S(1)}, u32[]{:S(2)}, u32[]{:S(2)}) %collective-permute-start.35) | collective-permute-done | bytes 544 | tf_op jit(solution)/shard_map/ppermute | solution.py:20
  186.1 3.9 %collective-permute-start.37 = (f32[42,1]{1,0:T(8,128)S(1)}, f32[42,1]{1,0:T(8,128)S(1)}, u32[]{:S(2)}, u32[]{:S(2)}) collective-permute-start(f32[42,1]{1,0:T(8,128)S(1)} %get-tuple-element.53), channel_id=1, source_target_pairs={{0,8},{8,16},{16,24},{1,9},{9,17},{17,25},{2,10},{10,18},{18,26},{... | collective-permute-start | bytes 512 | tf_op jit(solution)/shard_map/ppermute | solution.py:20
  190.0 2.7 %collective-permute-done.37 = f32[42,1]{1,0:T(8,128)S(1)} collective-permute-done((f32[42,1]{1,0:T(8,128)S(1)}, f32[42,1]{1,0:T(8,128)S(1)}, u32[]{:S(2)}, u32[]{:S(2)}) %collective-permute-start.37) | collective-permute-done | bytes 200 | tf_op jit(solution)/shard_map/ppermute | solution.py:20
  192.8 1.9 collective-permute-start.38
  196.0 4.2 %collective-permute-done.39 = f32[1,128]{1,0:T(1,128)S(1)} collective-permute-done((f32[1,128]{1,0:T(1,128)S(1)}, f32[1,128]{1,0:T(1,128)S(1)}, u32[]{:S(2)}, u32[]{:S(2)}) %collective-permute-start.39) | collective-permute-done | bytes 544 | tf_op jit(solution)/shard_map/ppermute | solution.py:20
  202.2 4.1 %collective-permute-start.41 = (f32[42,1]{1,0:T(8,128)S(1)}, f32[42,1]{1,0:T(8,128)S(1)}, u32[]{:S(2)}, u32[]{:S(2)}) collective-permute-start(f32[42,1]{1,0:T(8,128)S(1)} %get-tuple-element.51), channel_id=1, source_target_pairs={{0,8},{8,16},{16,24},{1,9},{9,17},{17,25},{2,10},{10,18},{18,26},{... | collective-permute-start | bytes 512 | tf_op jit(solution)/shard_map/ppermute | solution.py:20
  206.4 2.5 %collective-permute-done.41 = f32[42,1]{1,0:T(8,128)S(1)} collective-permute-done((f32[42,1]{1,0:T(8,128)S(1)}, f32[42,1]{1,0:T(8,128)S(1)}, u32[]{:S(2)}, u32[]{:S(2)}) %collective-permute-start.41) | collective-permute-done | bytes 200 | tf_op jit(solution)/shard_map/ppermute | solution.py:20
  (232 shorter events, 49.3 us)
Async XLA Ops:
  7.2 65.1 %all-reduce.4.cloned.1.call-start = ((), (), s32[]{:S(2)}) async-start(), calls=%async_computation | async-start | bytes 245760 | tf_op jit(solution)/shard_map/psum | solution.py:151
  8.5 28.1 %collective-permute-start.6 = (f32[1,128]{1,0:T(1,128)S(1)}, f32[1,128]{1,0:T(1,128)S(1)}, u32[]{:S(2)}, u32[]{:S(2)}) collective-permute-start(f32[1,128]{1,0:T(1,128)S(1)} %broadcast.60), channel_id=1, source_target_pairs={{2,0},{4,2},{6,4},{3,1},{5,3},{7,5},{10,8},{12,10},{14,12},{11,9},... | collective-permute-start | bytes 1544 | tf_op jit(solution)/shard_map/ppermute | solution.py:22
  10.8 25.7 %collective-permute-start.7 = (f32[1,128]{1,0:T(1,128)S(1)}, f32[1,128]{1,0:T(1,128)S(1)}, u32[]{:S(2)}, u32[]{:S(2)}) collective-permute-start(f32[1,128]{1,0:T(1,128)S(1)} %broadcast.60), channel_id=1, source_target_pairs={{0,2},{2,4},{4,6},{1,3},{3,5},{5,7},{8,10},{10,12},{12,14},{9,11},... | collective-permute-start | bytes 1544 | tf_op jit(solution)/shard_map/ppermute | solution.py:20
  12.2 4.0 %collective-permute-start = (f32[4,1,40,128]{3,2,1,0:T(8,128)S(1)}, f32[4,1,40,128]{3,2,1,0:T(8,128)S(1)}, u32[]{:S(2)}, u32[]{:S(2)}) collective-permute-start(f32[4,1,40,128]{3,2,1,0:T(8,128)S(1)} %get-tuple-element.34), channel_id=1, source_target_pairs={{0,1},{2,3},{4,5},{6,7},{8,9},{10,11},{12,13},{14,15},{16,17},{18,... | collective-permute-start | bytes 245768 | tf_op jit(solution)/shard_map/ppermute | solution.py:20
  13.7 3.2 %collective-permute-start.1 = (f32[4,1,40,128]{3,2,1,0:T(8,128)S(1)}, f32[4,1,40,128]{3,2,1,0:T(8,128)S(1)}, u32[]{:S(2)}, u32[]{:S(2)}) collective-permute-start(f32[4,1,40,128]{3,2,1,0:T(8,128)S(1)} %get-tuple-element.35), channel_id=1, source_target_pairs={{1,0},{3,2},{5,4},{7,6},{9,8},{11,10},{13,12},{15,14},{17,16},{19,... | collective-permute-start | bytes 245768 | tf_op jit(solution)/shard_map/ppermute | solution.py:22
  16.9 6.9 %collective-permute-start.2 = (f32[4,18,1,128]{3,0,2,1:T(4,128)S(1)}, f32[4,18,1,128]{3,0,2,1:T(4,128)S(1)}, u32[]{:S(2)}, u32[]{:S(2)}) collective-permute-start(f32[4,18,1,128]{3,0,2,1:T(4,128)S(1)} %copy.244), channel_id=1, source_target_pairs={{0,2},{2,4},{4,6},{1,3},{3,5},{5,7},{8,10},{10,12},{12,14},{9,11},... | collective-permute-start | bytes 110600 | tf_op jit(solution)/shard_map/ppermute | solution.py:20
  18.2 6.6 %collective-permute-start.3 = (f32[4,18,1,128]{3,0,2,1:T(4,128)S(1)}, f32[4,18,1,128]{3,0,2,1:T(4,128)S(1)}, u32[]{:S(2)}, u32[]{:S(2)}) collective-permute-start(f32[4,18,1,128]{3,0,2,1:T(4,128)S(1)} %copy.245), channel_id=1, source_target_pairs={{2,0},{4,2},{6,4},{3,1},{5,3},{7,5},{10,8},{12,10},{14,12},{11,9},... | collective-permute-start | bytes 110600 | tf_op jit(solution)/shard_map/ppermute | solution.py:22
  29.1 7.5 %collective-permute-start.4 = (f32[4,18,42,1]{2,0,3,1:T(4,128)S(1)}, f32[4,18,42,1]{2,0,3,1:T(4,128)S(1)}, u32[]{:S(2)}, u32[]{:S(2)}) collective-permute-start(f32[4,18,42,1]{2,0,3,1:T(4,128)S(1)} %copy.218), channel_id=1, source_target_pairs={{0,8},{8,16},{16,24},{1,9},{9,17},{17,25},{2,10},{10,18},{18,26},{... | collective-permute-start | bytes 36296 | tf_op jit(solution)/shard_map/ppermute | solution.py:20
  33.2 5.8 %collective-permute-start.5 = (f32[4,18,42,1]{2,0,3,1:T(4,128)S(1)}, f32[4,18,42,1]{2,0,3,1:T(4,128)S(1)}, u32[]{:S(2)}, u32[]{:S(2)}) collective-permute-start(f32[4,18,42,1]{2,0,3,1:T(4,128)S(1)} %copy.219), channel_id=1, source_target_pairs={{8,0},{16,8},{24,16},{9,1},{17,9},{25,17},{10,2},{18,10},{26,18},{... | collective-permute-start | bytes 36296 | tf_op jit(solution)/shard_map/ppermute | solution.py:22
  51.7 6.2 %collective-permute-start.8 = (f32[42,1]{1,0:T(8,128)S(1)}, f32[42,1]{1,0:T(8,128)S(1)}, u32[]{:S(2)}, u32[]{:S(2)}) collective-permute-start(f32[42,1]{1,0:T(8,128)S(1)} %get-tuple-element.66), channel_id=1, source_target_pairs={{8,0},{16,8},{24,16},{9,1},{17,9},{25,17},{10,2},{18,10},{26,18},{... | collective-permute-start | bytes 512 | tf_op jit(solution)/shard_map/ppermute | solution.py:22
  56.0 6.6 %collective-permute-start.9 = (f32[42,1]{1,0:T(8,128)S(1)}, f32[42,1]{1,0:T(8,128)S(1)}, u32[]{:S(2)}, u32[]{:S(2)}) collective-permute-start(f32[42,1]{1,0:T(8,128)S(1)} %get-tuple-element.67), channel_id=1, source_target_pairs={{0,8},{8,16},{16,24},{1,9},{9,17},{17,25},{2,10},{10,18},{18,26},{... | collective-permute-start | bytes 512 | tf_op jit(solution)/shard_map/ppermute | solution.py:20
  73.3 3.9 %collective-permute-start.10 = (f32[1,128]{1,0:T(1,128)S(1)}, f32[1,128]{1,0:T(1,128)S(1)}, u32[]{:S(2)}, u32[]{:S(2)}) collective-permute-start(f32[1,128]{1,0:T(1,128)S(1)} %get-tuple-element.87), channel_id=1, source_target_pairs={{2,0},{4,2},{6,4},{3,1},{5,3},{7,5},{10,8},{12,10},{14,12},{11,9},... | collective-permute-start | bytes 1544 | tf_op jit(solution)/shard_map/ppermute | solution.py:22
  75.7 133.2 %copy-start.4 = (f32[16,40,128]{2,1,0:T(8,128)S(1)}, f32[16,40,128]{2,1,0:T(8,128)}, u32[]{:S(2)}) copy-start(f32[16,40,128]{2,1,0:T(8,128)} %copy-done.3) | copy-start | bytes 983044
  75.7 133.2 %copy-start.6 = (f32[16,40,128]{2,1,0:T(8,128)S(1)}, f32[16,40,128]{2,1,0:T(8,128)}, u32[]{:S(2)}) copy-start(f32[16,40,128]{2,1,0:T(8,128)} %copy-done.5) | copy-start | bytes 983044
  75.7 133.2 %copy-start.8 = (f32[16,40,128]{2,1,0:T(8,128)S(1)}, f32[16,40,128]{2,1,0:T(8,128)}, u32[]{:S(2)}) copy-start(f32[16,40,128]{2,1,0:T(8,128)} %copy-done.7) | copy-start | bytes 983044
  75.7 133.2 %copy-start.10 = (f32[16,40,128]{2,1,0:T(8,128)S(1)}, f32[16,40,128]{2,1,0:T(8,128)}, u32[]{:S(2)}) copy-start(f32[16,40,128]{2,1,0:T(8,128)} %copy-done.9) | copy-start | bytes 983044
  75.7 133.2 %copy-start.26 = (f32[16]{0:T(128)S(1)}, f32[16]{0:T(128)}, u32[]{:S(2)}) copy-start(f32[16]{0:T(128)} %get-tuple-element.88) | copy-start | bytes 196
  75.8 5.6 %collective-permute-start.11 = (f32[1,128]{1,0:T(1,128)S(1)}, f32[1,128]{1,0:T(1,128)S(1)}, u32[]{:S(2)}, u32[]{:S(2)}) collective-permute-start(f32[1,128]{1,0:T(1,128)S(1)} %get-tuple-element.86), channel_id=1, source_target_pairs={{0,2},{2,4},{4,6},{1,3},{3,5},{5,7},{8,10},{10,12},{12,14},{9,11},... | collective-permute-start | bytes 1544 | tf_op jit(solution)/shard_map/ppermute | solution.py:20
  81.4 5.8 %collective-permute-start.12 = (f32[42,1]{1,0:T(8,128)S(1)}, f32[42,1]{1,0:T(8,128)S(1)}, u32[]{:S(2)}, u32[]{:S(2)}) collective-permute-start(f32[42,1]{1,0:T(8,128)S(1)} %get-tuple-element.64), channel_id=1, source_target_pairs={{8,0},{16,8},{24,16},{9,1},{17,9},{25,17},{10,2},{18,10},{26,18},{... | collective-permute-start | bytes 512 | tf_op jit(solution)/shard_map/ppermute | solution.py:22
  84.8 6.6 %collective-permute-start.13 = (f32[42,1]{1,0:T(8,128)S(1)}, f32[42,1]{1,0:T(8,128)S(1)}, u32[]{:S(2)}, u32[]{:S(2)}) collective-permute-start(f32[42,1]{1,0:T(8,128)S(1)} %get-tuple-element.65), channel_id=1, source_target_pairs={{0,8},{8,16},{16,24},{1,9},{9,17},{17,25},{2,10},{10,18},{18,26},{... | collective-permute-start | bytes 512 | tf_op jit(solution)/shard_map/ppermute | solution.py:20
  92.3 3.8 %collective-permute-start.14 = (f32[1,128]{1,0:T(1,128)S(1)}, f32[1,128]{1,0:T(1,128)S(1)}, u32[]{:S(2)}, u32[]{:S(2)}) collective-permute-start(f32[1,128]{1,0:T(1,128)S(1)} %get-tuple-element.85), channel_id=1, source_target_pairs={{2,0},{4,2},{6,4},{3,1},{5,3},{7,5},{10,8},{12,10},{14,12},{11,9},... | collective-permute-start | bytes 1544 | tf_op jit(solution)/shard_map/ppermute | solution.py:22
  94.8 5.5 %collective-permute-start.15 = (f32[1,128]{1,0:T(1,128)S(1)}, f32[1,128]{1,0:T(1,128)S(1)}, u32[]{:S(2)}, u32[]{:S(2)}) collective-permute-start(f32[1,128]{1,0:T(1,128)S(1)} %get-tuple-element.84), channel_id=1, source_target_pairs={{0,2},{2,4},{4,6},{1,3},{3,5},{5,7},{8,10},{10,12},{12,14},{9,11},... | collective-permute-start | bytes 1544 | tf_op jit(solution)/shard_map/ppermute | solution.py:20
  100.4 5.8 %collective-permute-start.16 = (f32[42,1]{1,0:T(8,128)S(1)}, f32[42,1]{1,0:T(8,128)S(1)}, u32[]{:S(2)}, u32[]{:S(2)}) collective-permute-start(f32[42,1]{1,0:T(8,128)S(1)} %get-tuple-element.62), channel_id=1, source_target_pairs={{8,0},{16,8},{24,16},{9,1},{17,9},{25,17},{10,2},{18,10},{26,18},{... | collective-permute-start | bytes 512 | tf_op jit(solution)/shard_map/ppermute | solution.py:22
  102.3 6.6 %collective-permute-start.17 = (f32[42,1]{1,0:T(8,128)S(1)}, f32[42,1]{1,0:T(8,128)S(1)}, u32[]{:S(2)}, u32[]{:S(2)}) collective-permute-start(f32[42,1]{1,0:T(8,128)S(1)} %get-tuple-element.63), channel_id=1, source_target_pairs={{0,8},{8,16},{16,24},{1,9},{9,17},{17,25},{2,10},{10,18},{18,26},{... | collective-permute-start | bytes 512 | tf_op jit(solution)/shard_map/ppermute | solution.py:20
  109.8 3.8 %collective-permute-start.18 = (f32[1,128]{1,0:T(1,128)S(1)}, f32[1,128]{1,0:T(1,128)S(1)}, u32[]{:S(2)}, u32[]{:S(2)}) collective-permute-start(f32[1,128]{1,0:T(1,128)S(1)} %get-tuple-element.83), channel_id=1, source_target_pairs={{2,0},{4,2},{6,4},{3,1},{5,3},{7,5},{10,8},{12,10},{14,12},{11,9},... | collective-permute-start | bytes 1544 | tf_op jit(solution)/shard_map/ppermute | solution.py:22
  112.3 5.5 %collective-permute-start.19 = (f32[1,128]{1,0:T(1,128)S(1)}, f32[1,128]{1,0:T(1,128)S(1)}, u32[]{:S(2)}, u32[]{:S(2)}) collective-permute-start(f32[1,128]{1,0:T(1,128)S(1)} %get-tuple-element.82), channel_id=1, source_target_pairs={{0,2},{2,4},{4,6},{1,3},{3,5},{5,7},{8,10},{10,12},{12,14},{9,11},... | collective-permute-start | bytes 1544 | tf_op jit(solution)/shard_map/ppermute | solution.py:20
  117.8 5.8 %collective-permute-start.20 = (f32[42,1]{1,0:T(8,128)S(1)}, f32[42,1]{1,0:T(8,128)S(1)}, u32[]{:S(2)}, u32[]{:S(2)}) collective-permute-start(f32[42,1]{1,0:T(8,128)S(1)} %get-tuple-element.60), channel_id=1, source_target_pairs={{8,0},{16,8},{24,16},{9,1},{17,9},{25,17},{10,2},{18,10},{26,18},{... | collective-permute-start | bytes 512 | tf_op jit(solution)/shard_map/ppermute | solution.py:22
  119.7 6.6 %collective-permute-start.21 = (f32[42,1]{1,0:T(8,128)S(1)}, f32[42,1]{1,0:T(8,128)S(1)}, u32[]{:S(2)}, u32[]{:S(2)}) collective-permute-start(f32[42,1]{1,0:T(8,128)S(1)} %get-tuple-element.61), channel_id=1, source_target_pairs={{0,8},{8,16},{16,24},{1,9},{9,17},{17,25},{2,10},{10,18},{18,26},{... | collective-permute-start | bytes 512 | tf_op jit(solution)/shard_map/ppermute | solution.py:20
  127.3 3.2 %collective-permute-start.22 = (f32[1,128]{1,0:T(1,128)S(1)}, f32[1,128]{1,0:T(1,128)S(1)}, u32[]{:S(2)}, u32[]{:S(2)}) collective-permute-start(f32[1,128]{1,0:T(1,128)S(1)} %get-tuple-element.81), channel_id=1, source_target_pairs={{2,0},{4,2},{6,4},{3,1},{5,3},{7,5},{10,8},{12,10},{14,12},{11,9},... | collective-permute-start | bytes 1544 | tf_op jit(solution)/shard_map/ppermute | solution.py:22
  129.2 5.5 %collective-permute-start.23 = (f32[1,128]{1,0:T(1,128)S(1)}, f32[1,128]{1,0:T(1,128)S(1)}, u32[]{:S(2)}, u32[]{:S(2)}) collective-permute-start(f32[1,128]{1,0:T(1,128)S(1)} %get-tuple-element.80), channel_id=1, source_target_pairs={{0,2},{2,4},{4,6},{1,3},{3,5},{5,7},{8,10},{10,12},{12,14},{9,11},... | collective-permute-start | bytes 1544 | tf_op jit(solution)/shard_map/ppermute | solution.py:20
  134.8 5.8 %collective-permute-start.24 = (f32[42,1]{1,0:T(8,128)S(1)}, f32[42,1]{1,0:T(8,128)S(1)}, u32[]{:S(2)}, u32[]{:S(2)}) collective-permute-start(f32[42,1]{1,0:T(8,128)S(1)} %get-tuple-element.58), channel_id=1, source_target_pairs={{8,0},{16,8},{24,16},{9,1},{17,9},{25,17},{10,2},{18,10},{26,18},{... | collective-permute-start | bytes 512 | tf_op jit(solution)/shard_map/ppermute | solution.py:22
  136.7 6.6 %collective-permute-start.25 = (f32[42,1]{1,0:T(8,128)S(1)}, f32[42,1]{1,0:T(8,128)S(1)}, u32[]{:S(2)}, u32[]{:S(2)}) collective-permute-start(f32[42,1]{1,0:T(8,128)S(1)} %get-tuple-element.59), channel_id=1, source_target_pairs={{0,8},{8,16},{16,24},{1,9},{9,17},{17,25},{2,10},{10,18},{18,26},{... | collective-permute-start | bytes 512 | tf_op jit(solution)/shard_map/ppermute | solution.py:20
  144.2 3.2 %collective-permute-start.26 = (f32[1,128]{1,0:T(1,128)S(1)}, f32[1,128]{1,0:T(1,128)S(1)}, u32[]{:S(2)}, u32[]{:S(2)}) collective-permute-start(f32[1,128]{1,0:T(1,128)S(1)} %get-tuple-element.79), channel_id=1, source_target_pairs={{2,0},{4,2},{6,4},{3,1},{5,3},{7,5},{10,8},{12,10},{14,12},{11,9},... | collective-permute-start | bytes 1544 | tf_op jit(solution)/shard_map/ppermute | solution.py:22
  146.2 5.5 %collective-permute-start.27 = (f32[1,128]{1,0:T(1,128)S(1)}, f32[1,128]{1,0:T(1,128)S(1)}, u32[]{:S(2)}, u32[]{:S(2)}) collective-permute-start(f32[1,128]{1,0:T(1,128)S(1)} %get-tuple-element.78), channel_id=1, source_target_pairs={{0,2},{2,4},{4,6},{1,3},{3,5},{5,7},{8,10},{10,12},{12,14},{9,11},... | collective-permute-start | bytes 1544 | tf_op jit(solution)/shard_map/ppermute | solution.py:20
  151.7 5.8 %collective-permute-start.28 = (f32[42,1]{1,0:T(8,128)S(1)}, f32[42,1]{1,0:T(8,128)S(1)}, u32[]{:S(2)}, u32[]{:S(2)}) collective-permute-start(f32[42,1]{1,0:T(8,128)S(1)} %get-tuple-element.56), channel_id=1, source_target_pairs={{8,0},{16,8},{24,16},{9,1},{17,9},{25,17},{10,2},{18,10},{26,18},{... | collective-permute-start | bytes 512 | tf_op jit(solution)/shard_map/ppermute | solution.py:22
  153.6 6.6 %collective-permute-start.29 = (f32[42,1]{1,0:T(8,128)S(1)}, f32[42,1]{1,0:T(8,128)S(1)}, u32[]{:S(2)}, u32[]{:S(2)}) collective-permute-start(f32[42,1]{1,0:T(8,128)S(1)} %get-tuple-element.57), channel_id=1, source_target_pairs={{0,8},{8,16},{16,24},{1,9},{9,17},{17,25},{2,10},{10,18},{18,26},{... | collective-permute-start | bytes 512 | tf_op jit(solution)/shard_map/ppermute | solution.py:20
  160.4 3.2 %collective-permute-start.30 = (f32[1,128]{1,0:T(1,128)S(1)}, f32[1,128]{1,0:T(1,128)S(1)}, u32[]{:S(2)}, u32[]{:S(2)}) collective-permute-start(f32[1,128]{1,0:T(1,128)S(1)} %get-tuple-element.77), channel_id=1, source_target_pairs={{2,0},{4,2},{6,4},{3,1},{5,3},{7,5},{10,8},{12,10},{14,12},{11,9},... | collective-permute-start | bytes 1544 | tf_op jit(solution)/shard_map/ppermute | solution.py:22
  162.3 5.5 %collective-permute-start.31 = (f32[1,128]{1,0:T(1,128)S(1)}, f32[1,128]{1,0:T(1,128)S(1)}, u32[]{:S(2)}, u32[]{:S(2)}) collective-permute-start(f32[1,128]{1,0:T(1,128)S(1)} %get-tuple-element.76), channel_id=1, source_target_pairs={{0,2},{2,4},{4,6},{1,3},{3,5},{5,7},{8,10},{10,12},{12,14},{9,11},... | collective-permute-start | bytes 1544 | tf_op jit(solution)/shard_map/ppermute | solution.py:20
  167.8 5.8 %collective-permute-start.32 = (f32[42,1]{1,0:T(8,128)S(1)}, f32[42,1]{1,0:T(8,128)S(1)}, u32[]{:S(2)}, u32[]{:S(2)}) collective-permute-start(f32[42,1]{1,0:T(8,128)S(1)} %get-tuple-element.54), channel_id=1, source_target_pairs={{8,0},{16,8},{24,16},{9,1},{17,9},{25,17},{10,2},{18,10},{26,18},{... | collective-permute-start | bytes 512 | tf_op jit(solution)/shard_map/ppermute | solution.py:22
  169.7 6.7 %collective-permute-start.33 = (f32[42,1]{1,0:T(8,128)S(1)}, f32[42,1]{1,0:T(8,128)S(1)}, u32[]{:S(2)}, u32[]{:S(2)}) collective-permute-start(f32[42,1]{1,0:T(8,128)S(1)} %get-tuple-element.55), channel_id=1, source_target_pairs={{0,8},{8,16},{16,24},{1,9},{9,17},{17,25},{2,10},{10,18},{18,26},{... | collective-permute-start | bytes 512 | tf_op jit(solution)/shard_map/ppermute | solution.py:20
  176.5 3.4 %collective-permute-start.34 = (f32[1,128]{1,0:T(1,128)S(1)}, f32[1,128]{1,0:T(1,128)S(1)}, u32[]{:S(2)}, u32[]{:S(2)}) collective-permute-start(f32[1,128]{1,0:T(1,128)S(1)} %get-tuple-element.75), channel_id=1, source_target_pairs={{2,0},{4,2},{6,4},{3,1},{5,3},{7,5},{10,8},{12,10},{14,12},{11,9},... | collective-permute-start | bytes 1544 | tf_op jit(solution)/shard_map/ppermute | solution.py:22
  178.6 5.5 %collective-permute-start.35 = (f32[1,128]{1,0:T(1,128)S(1)}, f32[1,128]{1,0:T(1,128)S(1)}, u32[]{:S(2)}, u32[]{:S(2)}) collective-permute-start(f32[1,128]{1,0:T(1,128)S(1)} %get-tuple-element.74), channel_id=1, source_target_pairs={{0,2},{2,4},{4,6},{1,3},{3,5},{5,7},{8,10},{10,12},{12,14},{9,11},... | collective-permute-start | bytes 1544 | tf_op jit(solution)/shard_map/ppermute | solution.py:20
  184.1 5.8 %collective-permute-start.36 = (f32[42,1]{1,0:T(8,128)S(1)}, f32[42,1]{1,0:T(8,128)S(1)}, u32[]{:S(2)}, u32[]{:S(2)}) collective-permute-start(f32[42,1]{1,0:T(8,128)S(1)} %get-tuple-element.52), channel_id=1, source_target_pairs={{8,0},{16,8},{24,16},{9,1},{17,9},{25,17},{10,2},{18,10},{26,18},{... | collective-permute-start | bytes 512 | tf_op jit(solution)/shard_map/ppermute | solution.py:22
  186.1 6.6 %collective-permute-start.37 = (f32[42,1]{1,0:T(8,128)S(1)}, f32[42,1]{1,0:T(8,128)S(1)}, u32[]{:S(2)}, u32[]{:S(2)}) collective-permute-start(f32[42,1]{1,0:T(8,128)S(1)} %get-tuple-element.53), channel_id=1, source_target_pairs={{0,8},{8,16},{16,24},{1,9},{9,17},{17,25},{2,10},{10,18},{18,26},{... | collective-permute-start | bytes 512 | tf_op jit(solution)/shard_map/ppermute | solution.py:20
  192.8 3.2 %collective-permute-start.38 = (f32[1,128]{1,0:T(1,128)S(1)}, f32[1,128]{1,0:T(1,128)S(1)}, u32[]{:S(2)}, u32[]{:S(2)}) collective-permute-start(f32[1,128]{1,0:T(1,128)S(1)} %get-tuple-element.73), channel_id=1, source_target_pairs={{2,0},{4,2},{6,4},{3,1},{5,3},{7,5},{10,8},{12,10},{14,12},{11,9},... | collective-permute-start | bytes 1544 | tf_op jit(solution)/shard_map/ppermute | solution.py:22
  194.7 5.5 %collective-permute-start.39 = (f32[1,128]{1,0:T(1,128)S(1)}, f32[1,128]{1,0:T(1,128)S(1)}, u32[]{:S(2)}, u32[]{:S(2)}) collective-permute-start(f32[1,128]{1,0:T(1,128)S(1)} %get-tuple-element.72), channel_id=1, source_target_pairs={{0,2},{2,4},{4,6},{1,3},{3,5},{5,7},{8,10},{10,12},{12,14},{9,11},... | collective-permute-start | bytes 1544 | tf_op jit(solution)/shard_map/ppermute | solution.py:20
  200.3 6.1 %collective-permute-start.40 = (f32[42,1]{1,0:T(8,128)S(1)}, f32[42,1]{1,0:T(8,128)S(1)}, u32[]{:S(2)}, u32[]{:S(2)}) collective-permute-start(f32[42,1]{1,0:T(8,128)S(1)} %get-tuple-element.50), channel_id=1, source_target_pairs={{8,0},{16,8},{24,16},{9,1},{17,9},{25,17},{10,2},{18,10},{26,18},{... | collective-permute-start | bytes 512 | tf_op jit(solution)/shard_map/ppermute | solution.py:22
  202.2 6.6 %collective-permute-start.41 = (f32[42,1]{1,0:T(8,128)S(1)}, f32[42,1]{1,0:T(8,128)S(1)}, u32[]{:S(2)}, u32[]{:S(2)}) collective-permute-start(f32[42,1]{1,0:T(8,128)S(1)} %get-tuple-element.51), channel_id=1, source_target_pairs={{0,8},{8,16},{16,24},{1,9},{9,17},{17,25},{2,10},{10,18},{18,26},{... | collective-permute-start | bytes 512 | tf_op jit(solution)/shard_map/ppermute | solution.py:20
  (45 other events, 249.8 us)
Sparse Core Ops, SparseCore 0:
  51.8 20.4 all-reduce.3
where the time goes:
time: 223 us; the launch traced here: 221 us
  starting transfers between devices  100 us (45%)
  waiting for transfers between devices  73.7 us (33%)
  other arithmetic  16.3 us (7%)
  between operations  15.4 us (7%)
  local copies, waits for them, and re-layouts  15.1 us (7%)
    ppermute x21, waiting for transfers between devices, extended(): lax.ppermute(tail, axis, [(i, (i + 1) % count) for i in range(ends)])  60.6 us
    ppermute x21, starting transfers between devices, extended(): lax.ppermute(head, axis, [((i + 1) % count, i) for i in range(ends)])  50 us
    ppermute x21, starting transfers between devices, extended(): lax.ppermute(tail, axis, [(i, (i + 1) % count) for i in range(ends)])  49.9 us
    psum x1, waiting for transfers between devices, per_device(): totals = lax.psum(planes, 'gz')  9.72 us
    unnamed x116, local copies, waits for them, and re-layouts  5.28 us
  transfers between devices with their start and end apart: 43, of which 21 were waited for; matrix products, arithmetic and copies ran while one was open for 4% of the time, Pallas kernels for 0%

commit v1 on v0

v1 whole, which is shorter than its diff:
```python
import functools
import jax
import jax.numpy as jnp
from jax import lax
from jax.experimental import pallas as pl
from jax.experimental.pallas import tpu as pltpu
from jax.sharding import PartitionSpec as P

SWEEPS = 8
RELAX = 0.8
MESH = pl.DeviceIdType.MESH
HALO = 8
LANES = 128

PLANES = 4
SIDES = [(-1, 0), (1, 0), (0, -1), (0, 1), (-1, -1), (-1, 1), (1, -1), (1, 1)]


def face(a, b):
    return 2.0 * a * b / (a + b)


def kernel(sizes, facies, mtab, ktab, state_hbm, rhs_hbm, perm_hbm, pore_hbm,
           new_hbm, corr_ref,
           u, rhs, permb, poreb, ysend, yrecv, xsend, xrecv,
           flux, ty, txp, txm, tzs, tot, w, qv, zplanes, ext, cxsend, cxrecv, field,
           in_sem, out_sem, h_send, h_recv, z_send, z_recv, c_send, c_recv):
    ngx, ngy, ngz, nz, ny, nx = sizes
    ix, iy, iz = lax.axis_index("gx"), lax.axis_index("gy"), lax.axis_index("gz")
    own = slice(HALO, HALO + ny)

    loads = [
        pltpu.make_async_copy(perm_hbm, permb, in_sem.at[0]),
        pltpu.make_async_copy(state_hbm, u.at[0:3, 1:nz + 1, own], in_sem.at[1]),
        pltpu.make_async_copy(pore_hbm, poreb, in_sem.at[2]),
        pltpu.make_async_copy(rhs_hbm, rhs, in_sem.at[3]),
    ]
    for load in loads:
        load.start()

    def exists(dy, dx):
        ok = None
        for d, i, n in ((dy, iy, ngy), (dx, ix, ngx)):
            if d:
                here = (i > 0) if d < 0 else (i < n - 1)
                ok = here if ok is None else jnp.logical_and(ok, here)
        return ok

    def at(dy, dx):
        return {"gx": ix + dx, "gy": iy + dy, "gz": iz}

    barrier = pltpu.get_barrier_semaphore()
    for side in SIDES:
        @pl.when(exists(*side))
        def _(side=side):
            pl.semaphore_signal(barrier, inc=1, device_id=at(*side), device_id_type=MESH)
    for d in range(1, ngz):
        pl.semaphore_signal(barrier, inc=1, device_id={"gx": ix, "gy": iy, "gz": lax.rem(iz + d, ngz)},
                            device_id_type=MESH)

    lane = lax.broadcasted_iota(jnp.int32, (ny, nx), 1)

    def zero(ref):
        ref[...] = jnp.zeros(ref.shape, ref.dtype)

    for cond, refs in (
        (iz == 0, [u.at[:, 0, own]]),
        (iz == ngz - 1, [u.at[:, nz + 1, own]]),
        (iy == 0, [yrecv.at[0], ext.at[:, 0:HALO]]),
        (iy == ngy - 1, [yrecv.at[1], ext.at[:, HALO + ny:]]),
        (ix == 0, [xrecv.at[0], cxrecv.at[0, own]]),
        (ix == ngx - 1, [xrecv.at[1], cxrecv.at[1, own]]),
        (jnp.logical_or(iy == 0, ix == 0), [cxrecv.at[0, 0:HALO]]),
        (jnp.logical_or(iy == 0, ix == ngx - 1), [cxrecv.at[1, 0:HALO]]),
        (jnp.logical_or(iy == ngy - 1, ix == 0), [cxrecv.at[0, HALO + ny:]]),
        (jnp.logical_or(iy == ngy - 1, ix == ngx - 1), [cxrecv.at[1, HALO + ny:]]),
    ):
        @pl.when(cond)
        def _(refs=refs):
            for ref in refs:
                zero(ref)
    zero(field)

    loads[0].wait()

    def widen(z, _):
        u[3, z + 1, own, :] = permb[z].astype(jnp.float32)
        return 0

    lax.fori_loop(0, nz, widen, 0)
    loads[1].wait()

    def pack(z, packed):
        for k in range(4):
            slab = u[k, z + 1, own, :]
            j = k * nz + z
            ysend[0, pl.ds(j, 1), :] = u[k, z + 1, HALO:HALO + 1, :]
            ysend[1, pl.ds(j, 1), :] = u[k, z + 1, HALO + ny - 1:HALO + ny, :]
            packed = jnp.where(lax.shift_right_logical(lane, 1) == j,
                               pltpu.roll(slab, lax.rem(2 * j + 1, nx), 1), packed)
        return packed

    xsend[...] = lax.fori_loop(0, nz, pack, jnp.zeros((ny, nx), jnp.float32))

    count = sum(exists(*side).astype(jnp.int32) for side in SIDES) + (ngz - 1)
    pl.semaphore_wait(barrier, count)

    def remote(src, dst, send, recv, device):
        return pltpu.make_async_remote_copy(src_ref=src, dst_ref=dst, send_sem=send, recv_sem=recv,
                                            device_id=device, device_id_type=MESH)

    def z_device(d):
        return {"gx": ix, "gy": iy, "gz": iz + d}

    halos = [
        (iz < ngz - 1, iz > 0, remote(u.at[:, nz, own], u.at[:, 0, own], h_send.at[0], h_recv.at[0], z_device(1))),
        (iz > 0, iz < ngz - 1, remote(u.at[:, 1, own], u.at[:, nz + 1, own], h_send.at[1], h_recv.at[1], z_device(-1))),
        (exists(1, 0), exists(-1, 0), remote(ysend.at[1], yrecv.at[0], h_send.at[2], h_recv.at[2], at(1, 0))),
        (exists(-1, 0), exists(1, 0), remote(ysend.at[0], yrecv.at[1], h_send.at[3], h_recv.at[3], at(-1, 0))),
        (exists(0, 1), exists(0, -1), remote(xsend, xrecv.at[0], h_send.at[4], h_recv.at[4], at(0, 1))),
        (exists(0, -1), exists(0, 1), remote(xsend, xrecv.at[1], h_send.at[5], h_recv.at[5], at(0, -1))),
    ]

    def start(copies):
        for sends, _, copy in copies:
            @pl.when(sends)
            def _(copy=copy):
                copy.start()

    def wait_recv(copies):
        for _, gets, copy in copies:
            @pl.when(gets)
            def _(copy=copy):
                copy.wait_recv()

    def wait_send(copies):
        for sends, _, copy in copies:
            @pl.when(sends)
            def _(copy=copy):
                copy.wait_send()

    start(halos[4:])
    start(halos[2:4])
    start(halos[:2])
    loads[2].wait()
    loads[3].wait()
    wait_recv(halos)

    left = xrecv[0]
    border = jnp.where(lax.rem(lane, 2) == 0, left, pltpu.roll(xrecv[1], nx - 2, 1))
    mine = pltpu.roll(xsend[...], nx - 1, 1)
    left_t = jnp.where(lane >= 6 * nz, face(jnp.where(lane >= 6 * nz, left, 1.0), jnp.where(lane >= 6 * nz, mine, 1.0)), 0.0)
    first, last = lane == 0, lane == nx - 1

    def coefficient(table, z, r, c):
        return table[facies[z], r, c]

    def assemble(z, carry):
        tzm, s_rhs, s_diag, s_ty, s_tx = carry
        for k in range(4):
            j = k * nz + z
            u[k, z + 1, HALO - 1:HALO, :] = yrecv[0, pl.ds(j, 1), :]
            u[k, z + 1, HALO + ny:HALO + ny + 1, :] = yrecv[1, pl.ds(j, 1), :]

        def around(k):
            c = u[k, z + 1, own, :]
            h = pltpu.roll(border, lax.rem(2 * nx - 2 * (k * nz + z), nx), 1)
            return (c, u[k, z + 2, own, :], u[k, z, own, :],
                    u[k, z + 1, HALO + 1:HALO + ny + 1, :], u[k, z + 1, HALO - 1:HALO + ny - 1, :],
                    jnp.where(last, h, pltpu.roll(c, nx - 1, 1)), jnp.where(first, h, pltpu.roll(c, 1, 1)))

        q, qzp, _, qyp, _, qxp, _ = around(3)
        tzp = face(q, qzp)
        typ = face(q, qyp)
        ty[z, own, :] = typ
        ty[z, HALO - 1:HALO, :] = face(u[3, z + 1, HALO - 1:HALO, :], u[3, z + 1, HALO:HALO + 1, :])
        tym = ty[z, HALO - 1:HALO + ny - 1, :]
        xp = face(q, qxp)
        xm = jnp.where(first, pltpu.roll(left_t, lax.rem(2 * nx - 2 * (3 * nz + z), nx), 1), pltpu.roll(xp, 1, 1))
        txp[z] = xp
        txm[z] = xm
        tz = tzp + tzm
        areal = typ + tym + xp + xm
        tzs[z] = tz
        tot[z] = tz + areal
        v = poreb[z].astype(jnp.float32)
        local, moved = 0.0, 0.0
        for k in range(3):
            c, zp, zm, yp, ym, cxp, cxm = around(k)
            f = (tzp * (c - zp) + tzm * (c - zm) + typ * (c - yp) + tym * (c - ym)
                 + xp * (c - cxp) + xm * (c - cxm))
            flux[k, z] = f
            local = local + coefficient(mtab, z, 0, k) * c
            moved = moved + coefficient(ktab, z, 0, k) * f
        res = rhs[0, z] - (v * local + moved)
        rhs[0, z] = res
        k00 = coefficient(ktab, z, 0, 0)
        return (tzp, s_rhs + res, s_diag + (v * coefficient(mtab, z, 0, 0) + k00 * areal),
                s_ty + k00 * typ, s_tx + k00 * xp)

    nil = jnp.zeros((ny, nx), jnp.float32)
    carry = lax.fori_loop(0, nz, assemble, (face(u[3, 1, own, :], u[3, 0, own, :]), nil, nil, nil, nil))
    for p in range(PLANES):
        zplanes[iz, p] = carry[p + 1]

    others = [lax.rem(iz + d, ngz) for d in range(1, ngz)]
    sums = [remote(zplanes.at[iz], zplanes.at[iz], z_send.at[d], z_recv.at[iz], {"gx": ix, "gy": iy, "gz": peer})
            for d, peer in enumerate(others)]
    for copy in sums:
        copy.start()

    def solve(z, _):
        v = poreb[z].astype(jnp.float32)
        total = tot[z]
        m = [[coefficient(mtab, z, r, c) for c in range(3)] for r in range(3)]
        kk = [[coefficient(ktab, z, r, c) for c in range(3)] for r in range(3)]
        e = [[v * m[r][c] + total * kk[r][c] for c in range(3)] for r in range(3)]

        def cofactor(r, c):
            return (e[(r + 1) % 3][(c + 1) % 3] * e[(r + 2) % 3][(c + 2) % 3]
                    - e[(r + 1) % 3][(c + 2) % 3] * e[(r + 2) % 3][(c + 1) % 3])

        cells = [u[k, z + 1, own, :] for k in range(3)]
        f = [flux[k, z] for k in range(3)]
        res = [rhs[0, z]]
        for r in (1, 2):
            res.append(rhs[r, z] - (v * (m[r][0] * cells[0] + m[r][1] * cells[1] + m[r][2] * cells[2])
                                    + (kk[r][0] * f[0] + kk[r][1] * f[1] + kk[r][2] * f[2])))
        fac = [[cofactor(r, c) for c in range(3)] for r in range(3)]
        inv = 1.0 / (e[0][0] * fac[0][0] + e[0][1] * fac[0][1] + e[0][2] * fac[0][2])
        for r in range(3):
            w[r, z] = cells[r] + (fac[0][r] * res[0] + fac[1][r] * res[1] + fac[2][r] * res[2]) * inv
            qv[r, z] = (fac[0][r] * kk[0][0] + fac[1][r] * kk[1][0] + fac[2][r] * kk[2][0]) * inv
        return 0

    half = nz // 4
    lax.fori_loop(0, half, solve, 0)

    for peer in others:
        remote(zplanes.at[peer], zplanes.at[peer], z_send.at[0], z_recv.at[peer],
               {"gx": ix, "gy": iy, "gz": peer}).wait_recv()
    packed = nil
    for p in range(PLANES):
        plane = zplanes[0, p]
        for i in range(1, ngz):
            plane = plane + zplanes[i, p]
        ext[p, own, :] = plane
        packed = jnp.where(lax.shift_right_logical(lane, 4) == p, pltpu.roll(plane, 2 * HALO * p + HALO, 1), packed)
    cxsend[...] = packed

    low, high = slice(0, HALO), slice(ny - HALO, ny)
    elow, ehigh = slice(0, HALO), slice(HALO + ny, 2 * HALO + ny)
    coarse = []
    for s, (dy, dx) in enumerate(SIDES):
        rows = low if dy < 0 else high
        into = ehigh if dy < 0 else elow
        if dx == 0:
            src, dst = ext.at[:, slice(rows.start + HALO, rows.stop + HALO)], ext.at[:, into]
        elif dy == 0:
            src, dst = cxsend, cxrecv.at[0 if dx > 0 else 1, own]
        else:
            src, dst = cxsend.at[rows], cxrecv.at[0 if dx > 0 else 1, into]
        coarse.append((exists(dy, dx), exists(-dy, -dx), remote(src, dst, c_send.at[s], c_recv.at[s], at(dy, dx))))
    start(coarse)
    lax.fori_loop(half, nz, solve, 0)
    wait_recv(coarse)

    rows = ny + 2 * HALO
    elane = lax.broadcasted_iota(jnp.int32, (rows, nx), 1)
    efirst, elast = elane == 0, elane == nx - 1
    near = jnp.logical_or(elane < HALO, elane >= nx - HALO)
    beside = jnp.where(lax.rem(elane, 2 * HALO) < HALO, cxrecv[0], cxrecv[1])
    a = [ext[p] for p in range(PLANES)]
    b = [jnp.where(near, pltpu.roll(beside, nx - (2 * HALO * p + HALO), 1), 0.0) for p in range(PLANES)]

    def east(a, b):
        ra, rb = pltpu.roll(a, nx - 1, 1), pltpu.roll(b, nx - 1, 1)
        return jnp.where(elast, rb, ra), jnp.where(elast, ra, rb)

    def west(a, b):
        ra, rb = pltpu.roll(a, 1, 1), pltpu.roll(b, 1, 1)
        return jnp.where(efirst, rb, ra), jnp.where(efirst, ra, rb)

    mid = slice(HALO, HALO + rows)
    wests = west(a[3], b[3])
    terms = []
    for s, planes in enumerate((a, b)):
        there = planes[1] > 0.0
        inv = jnp.where(there, RELAX / jnp.where(there, planes[1], 1.0), 0.0)
        field[s, mid, :] = planes[2]
        south = field[s, HALO - 1:HALO - 1 + rows, :]
        terms.append((planes[0] * inv, planes[2] * inv, south * inv, planes[3] * inv, wests[s] * inv))

    c = [terms[0][0], terms[1][0]]
    for sweep in range(1, SWEEPS):
        e, ws = east(*c), west(*c)
        for s in range(2):
            field[s, mid, :] = c[s]
        nxt = []
        for s in range(2):
            r, tyn, tys, txe, txw = terms[s]
            nxt.append((1.0 - RELAX) * c[s] + r
                       + tyn * field[s, HALO + 1:HALO + 1 + rows, :] + tys * field[s, HALO - 1:HALO - 1 + rows, :]
                       + txe * e[s] + txw * ws[s])
        c = nxt
    e, ws = east(*c), west(*c)
    field[0, mid, :] = c[0]
    field[1, mid, :] = e[0]
    base = 2 * HALO
    ce = field[1, base:base + ny, :]
    field[1, mid, :] = ws[0]
    cw = field[1, base:base + ny, :]
    cc = field[0, base:base + ny, :]
    cn, cs = field[0, base + 1:base + 1 + ny, :], field[0, base - 1:base - 1 + ny, :]
    corr_ref[...] = cc

    def finish(z, _):
        g = (tzs[z] * cc + ty[z, own, :] * cn + ty[z, HALO - 1:HALO + ny - 1, :] * cs
             + txp[z] * ce + txm[z] * cw)
        for r in range(3):
            w[r, z] = w[r, z] + qv[r, z] * g
        return 0

    parts = 4
    step = nz // parts
    outs = []
    for part in range(parts):
        lax.fori_loop(part * step, (part + 1) * step, finish, 0)
        chunk = slice(part * step, (part + 1) * step)
        outs.append(pltpu.make_async_copy(w.at[:, chunk], new_hbm.at[:, chunk], out_sem.at[part]))
        outs[-1].start()
    wait_send(halos)
    for copy in sums:
        copy.wait_send()
    wait_send(coarse)
    for copy in outs:
        copy.wait()


def per_device(sizes, state, right_side, permeability, pore_volume, facies, storage_table, coupling_table):
    _, nz, ny, nx = state.shape
    sizes = sizes + (nz, ny, nx)
    f32 = jnp.float32
    ngz = sizes[2]
    cells = (nz, ny, nx)
    vmem = lambda *shape: pltpu.VMEM(shape, f32)
    anywhere = pl.BlockSpec(memory_space=pl.ANY)
    smem = pl.BlockSpec(memory_space=pltpu.SMEM)
    dma = lambda n: pltpu.SemaphoreType.DMA((n,))
    ey = ny + 2 * HALO
    return tuple(pl.pallas_call(
        functools.partial(kernel, sizes),
        out_shape=(jax.ShapeDtypeStruct(state.shape, f32), jax.ShapeDtypeStruct((ny, nx), f32)),
        in_specs=[smem, smem, smem, anywhere, anywhere, anywhere, anywhere],
        out_specs=(anywhere, pl.BlockSpec(memory_space=pltpu.VMEM)),
        scratch_shapes=[
            vmem(4, nz + 2, ey, nx), vmem(3, *cells),
            pltpu.VMEM(cells, permeability.dtype), pltpu.VMEM(cells, pore_volume.dtype),
            vmem(2, 4 * nz, nx), vmem(2, 4 * nz, nx), vmem(ny, nx), vmem(2, ny, nx),
            vmem(3, *cells), vmem(nz, ey, nx), vmem(*cells), vmem(*cells), vmem(*cells), vmem(*cells),
            vmem(3, *cells), vmem(3, *cells), vmem(ngz, PLANES, ny, nx), vmem(PLANES, ey, nx),
            vmem(ny, nx), vmem(2, ey, nx), vmem(2, ey + 2 * HALO, nx),
            dma(4), dma(4), dma(6), dma(6), dma(max(ngz - 1, 1)), dma(ngz), dma(8), dma(8),
        ],
        compiler_params=pltpu.CompilerParams(collective_id=0, has_side_effects=True),
        name="cpr_apply",
    )(facies, storage_table, coupling_table, state, right_side, permeability, pore_volume))


def solution(mesh):
    sizes = (mesh.shape["gx"], mesh.shape["gy"], mesh.shape["gz"])
    return jax.shard_map(
        functools.partial(per_device, sizes),
        mesh=mesh,
        in_specs=(
            P(None, "gz", "gy", "gx"),
            P(None, "gz", "gy", "gx"),
            P("gz", "gy", "gx"),
            P("gz", "gy", "gx"),
            P("gz"),
            P(),
            P(),
        ),
        out_specs=(P(None, "gz", "gy", "gx"), P("gy", "gx")),
        check_vma=False,
    )
```

time: 223 us -> 24.7 us (0.11)
  the two profiles are of different devices: /device:TPU:28 before, /device:TPU:0 now
where the time goes in v1:
time: 24.7 us; the launch traced here: 24.5 us
  Pallas kernels  19.1 us (77%)
  local copies, waits for them, and re-layouts  4.73 us (19%)
  between operations  0.66 us (3%)
    pallas_call x1, Pallas kernels, per_device(): pl.pallas_call(functools.partial(kernel, sizes), out_shape=(jax.ShapeDtyp...  19.1 us
    unnamed x8, local copies, waits for them, and re-layouts  4.73 us

profile of v1, /device:TPU:0, one launch (start us, length us, event | category | flops | bytes accessed | tf_op | source)
XLA Modules:
  0.0 24.5 jit_solution(3950194034855641877)
XLA Ops:
  0.6 0.0 copy-start.1
  0.6 1.3 %copy.9.mtab = f32[4,3,3]{2,1,0:T(4,128)} copy(f32[4,3,3]{2,0,1:T(4,128)} %param.12) | data formatting | bytes 288 | tf_op args[5]
  1.9 0.0 copy-done.1
  1.9 0.6 %copy.10.ktab = f32[4,3,3]{2,1,0:T(4,128)} copy(f32[4,3,3]{2,0,1:T(4,128)S(1)} %copy-done.1) | data formatting | bytes 288 | tf_op args[6]
  2.5 19.1 %cpr_apply.1 = (f32[3,16,40,128]{3,2,1,0:T(8,128)}, f32[40,128]{1,0:T(8,128)}) custom-call(s32[16]{0:T(128)} %facies.1, f32[4,3,3]{2,1,0:T(4,128)} %copy.9.mtab, f32[4,3,3]{2,1,0:T(4,128)} %copy.10.ktab, f32[3,16,40,128]{3,2,1,0:T(8,128)} %state_hbm.1, f32[3,16,40,128]{3,2,1,0:T(8,128)} %rhs_hbm.1, bf16[16,40,128]{2,1,0:T(8,128)(2,1)} %perm_hbm.1, ...), custom_call_target="tpu_custom_call" | custom-call | tf_op jit(solution)/shard_map/cpr_apply/pallas_call | solution.py:351
  21.7 0.0 copy-start
  21.7 2.2 %copy.13 = f32[3,16,40,128]{3,2,1,0:T(8,128)} copy(f32[3,16,40,128]{3,2,1,0:T(8,128)} %get-tuple-element.4) | data formatting | bytes 1966080
  23.9 0.0 copy-done
  23.9 0.6 %copy.14 = f32[40,128]{1,0:T(8,128)} copy(f32[40,128]{1,0:T(8,128)S(1)} %copy-done) | data formatting | bytes 40960
Async XLA Ops:
  0.6 1.3 %copy-start.1 = (f32[4,3,3]{2,0,1:T(4,128)S(1)}, f32[4,3,3]{2,0,1:T(4,128)}, u32[]{:S(2)}) copy-start(f32[4,3,3]{2,0,1:T(4,128)} %param.13) | copy-start | bytes 436
  21.7 2.2 %copy-start = (f32[40,128]{1,0:T(8,128)S(1)}, f32[40,128]{1,0:T(8,128)}, u32[]{:S(2)}) copy-start(f32[40,128]{1,0:T(8,128)} %get-tuple-element.5) | copy-start | bytes 61444

commit v2 on v1

--- a/solution.py
+++ b/solution.py
@@ -10,7 +10,7 @@
 RELAX = 0.8
 MESH = pl.DeviceIdType.MESH
 HALO = 8
-LANES = 128
+VMEM_BYTES = 67043328
 
 PLANES = 4
 SIDES = [(-1, 0), (1, 0), (0, -1), (0, 1), (-1, -1), (-1, 1), (1, -1), (1, 1)]
@@ -21,10 +21,10 @@
 
 
 def kernel(sizes, facies, mtab, ktab, state_hbm, rhs_hbm, perm_hbm, pore_hbm,
-           new_hbm, corr_ref,
+           w, qv, tzs, ty, txp, txm, final,
            u, rhs, permb, poreb, ysend, yrecv, xsend, xrecv,
-           flux, ty, txp, txm, tzs, tot, w, qv, zplanes, ext, cxsend, cxrecv, field,
-           in_sem, out_sem, h_send, h_recv, z_send, z_recv, c_send, c_recv):
+           flux, tot, zplanes, ext, cxsend, cxrecv, field,
+           in_sem, h_send, h_recv, z_send, z_recv, c_send, c_recv):
     ngx, ngy, ngz, nz, ny, nx = sizes
     ix, iy, iz = lax.axis_index("gx"), lax.axis_index("gy"), lax.axis_index("gz")
     own = slice(HALO, HALO + ny)
@@ -153,7 +153,7 @@
     first, last = lane == 0, lane == nx - 1
 
     def coefficient(table, z, r, c):
-        return table[facies[z], r, c]
+        return table[r, facies[z], c]
 
     def assemble(z, carry):
         tzm, s_rhs, s_diag, s_ty, s_tx = carry
@@ -304,35 +304,36 @@
                        + txe * e[s] + txw * ws[s])
         c = nxt
     e, ws = east(*c), west(*c)
-    field[0, mid, :] = c[0]
-    field[1, mid, :] = e[0]
-    base = 2 * HALO
-    ce = field[1, base:base + ny, :]
-    field[1, mid, :] = ws[0]
-    cw = field[1, base:base + ny, :]
-    cc = field[0, base:base + ny, :]
-    cn, cs = field[0, base + 1:base + 1 + ny, :], field[0, base - 1:base - 1 + ny, :]
+    final[0] = c[0]
+    final[1] = e[0]
+    final[2] = ws[0]
+    wait_send(halos)
+    for copy in sums:
+        copy.wait_send()
+    wait_send(coarse)
+
+
+def finish_kernel(parts, w, qv, tzs, ty, txp, txm, final, new_hbm, corr_ref, out, out_sem):
+    nz, ny, nx = tzs.shape
+    own = slice(HALO, HALO + ny)
+    cc, ce, cw = (final[k, own, :] for k in range(3))
+    cn, cs = final[0, HALO + 1:HALO + 1 + ny, :], final[0, HALO - 1:HALO - 1 + ny, :]
     corr_ref[...] = cc
 
     def finish(z, _):
         g = (tzs[z] * cc + ty[z, own, :] * cn + ty[z, HALO - 1:HALO + ny - 1, :] * cs
              + txp[z] * ce + txm[z] * cw)
         for r in range(3):
-            w[r, z] = w[r, z] + qv[r, z] * g
+            out[r, z] = w[r, z] + qv[r, z] * g
         return 0
 
-    parts = 4
     step = nz // parts
     outs = []
     for part in range(parts):
         lax.fori_loop(part * step, (part + 1) * step, finish, 0)
         chunk = slice(part * step, (part + 1) * step)
-        outs.append(pltpu.make_async_copy(w.at[:, chunk], new_hbm.at[:, chunk], out_sem.at[part]))
+        outs.append(pltpu.make_async_copy(out.at[:, chunk], new_hbm.at[:, chunk], out_sem.at[part]))
         outs[-1].start()
-    wait_send(halos)
-    for copy in sums:
-        copy.wait_send()
-    wait_send(coarse)
     for copy in outs:
         copy.wait()
 
@@ -344,27 +345,42 @@
     ngz = sizes[2]
     cells = (nz, ny, nx)
     vmem = lambda *shape: pltpu.VMEM(shape, f32)
-    anywhere = pl.BlockSpec(memory_space=pl.ANY)
+    hbm = pl.BlockSpec(memory_space=pltpu.HBM)
     smem = pl.BlockSpec(memory_space=pltpu.SMEM)
     dma = lambda n: pltpu.SemaphoreType.DMA((n,))
     ey = ny + 2 * HALO
-    return tuple(pl.pallas_call(
+    in_vmem = pl.BlockSpec(memory_space=pltpu.VMEM)
+    handed = 4 * nx * (9 * nz * ny + nz * ey + 3 * ey)
+    limit = 16384 * ((VMEM_BYTES - handed) // 16384)
+    middle = pl.pallas_call(
         functools.partial(kernel, sizes),
-        out_shape=(jax.ShapeDtypeStruct(state.shape, f32), jax.ShapeDtypeStruct((ny, nx), f32)),
-        in_specs=[smem, smem, smem, anywhere, anywhere, anywhere, anywhere],
-        out_specs=(anywhere, pl.BlockSpec(memory_space=pltpu.VMEM)),
+        out_shape=(vmem(3, *cells), vmem(3, *cells), vmem(*cells), vmem(nz, ey, nx), vmem(*cells), vmem(*cells),
+                   vmem(3, ey, nx)),
+        in_specs=[smem, smem, smem, hbm, hbm, hbm, hbm],
+        out_specs=(in_vmem,) * 7,
         scratch_shapes=[
             vmem(4, nz + 2, ey, nx), vmem(3, *cells),
             pltpu.VMEM(cells, permeability.dtype), pltpu.VMEM(cells, pore_volume.dtype),
             vmem(2, 4 * nz, nx), vmem(2, 4 * nz, nx), vmem(ny, nx), vmem(2, ny, nx),
-            vmem(3, *cells), vmem(nz, ey, nx), vmem(*cells), vmem(*cells), vmem(*cells), vmem(*cells),
-            vmem(3, *cells), vmem(3, *cells), vmem(ngz, PLANES, ny, nx), vmem(PLANES, ey, nx),
+            vmem(3, *cells), vmem(*cells),
+            vmem(ngz, PLANES, ny, nx), vmem(PLANES, ey, nx),
             vmem(ny, nx), vmem(2, ey, nx), vmem(2, ey + 2 * HALO, nx),
-            dma(4), dma(4), dma(6), dma(6), dma(max(ngz - 1, 1)), dma(ngz), dma(8), dma(8),
+            dma(4), dma(6), dma(6), dma(max(ngz - 1, 1)), dma(ngz), dma(8), dma(8),
         ],
-        compiler_params=pltpu.CompilerParams(collective_id=0, has_side_effects=True),
+        compiler_params=pltpu.CompilerParams(collective_id=0, has_side_effects=True, vmem_limit_bytes=limit),
         name="cpr_apply",
-    )(facies, storage_table, coupling_table, state, right_side, permeability, pore_volume))
+    )(facies, storage_table.transpose(1, 0, 2), coupling_table.transpose(1, 0, 2),
+      state, right_side, permeability, pore_volume)
+    parts = 4
+    return tuple(pl.pallas_call(
+        functools.partial(finish_kernel, parts),
+        out_shape=(jax.ShapeDtypeStruct(state.shape, f32), jax.ShapeDtypeStruct((ny, nx), f32)),
+        in_specs=[in_vmem] * 7,
+        out_specs=(hbm, in_vmem),
+        scratch_shapes=[vmem(3, *cells), dma(parts)],
+        compiler_params=pltpu.CompilerParams(vmem_limit_bytes=16 * 2**20),
+        name="cpr_finish",
+    )(*middle))
 
 
 def solution(mesh):

time: 24.7 us -> 19.9 us (0.81)
  local copies, waits for them, and re-layouts: 4.73 us -> 0 us
    unnamed x8 -> x0, local copies, waits for them, and re-layouts: 4.73 us -> none
    pallas_call x1 -> x2, Pallas kernels: 19.1 us -> 19.1 us  [the longest x1 17.4 us: per_device(): pl.pallas_call(functools.partial(kernel, sizes), out_shape=(vmem(3, *cell...]
where the time goes in v2:
time: 19.9 us; the launch traced here: 19.7 us
  Pallas kernels  19.1 us (96%)
  between operations  0.64 us (3%)
    pallas_call x1, Pallas kernels, per_device(): pl.pallas_call(functools.partial(kernel, sizes), out_shape=(vmem(3, *cell...  17.4 us
    pallas_call x1, Pallas kernels, per_device(): pl.pallas_call(functools.partial(finish_kernel, parts), out_shape=(jax.Sh...  1.65 us

profile of v2, /device:TPU:0, one launch (start us, length us, event | category | flops | bytes accessed | tf_op | source)
XLA Modules:
  0.0 19.7 jit_solution(9669832704177988382)
XLA Ops:
  0.6 17.4 %cpr_apply.1 = (f32[3,16,40,128]{3,2,1,0:T(8,128)S(1)}, f32[3,16,40,128]{3,2,1,0:T(8,128)S(1)}, f32[16,40,128]{2,1,0:T(8,128)S(1)}, f32[16,56,128]{2,1,0:T(8,128...) custom-call(s32[16]{0:T(128)} %facies.1, f32[3,4,3]{2,1,0:T(4,128)} %bitcast.2, ...), custom_call_target="tpu_custom_call" | custom-call | tf_op jit(solution)/shard_map/cpr_apply/pallas_call | solution.py:355
  18.1 1.6 %cpr_finish.1 = (f32[3,16,40,128]{3,2,1,0:T(8,128)}, f32[40,128]{1,0:T(8,128)}) custom-call(f32[3,16,40,128]{3,2,1,0:T(8,128)S(1)} %get-tuple-element.9.w, f32[3,16,40,128]{3,2,1,0:T(8,128)S(1)} %get-tuple-element.10.qv, f32[16,40,128]{2,1,0:T(8,128)S(1)} %get-tuple-element.11.tzs, f32[16,56,128]{2,1,0:T(8,128)S(1)} %get-tuple-element.12.ty, ...), custom_call_target="tpu_custom_call" | custom-call | tf_op jit(solution)/shard_map/cpr_finish/pallas_call | solution.py:375

commit v3 on v2

--- a/solution.py
+++ b/solution.py
@@ -22,7 +22,7 @@
 
 def kernel(sizes, facies, mtab, ktab, state_hbm, rhs_hbm, perm_hbm, pore_hbm,
            w, qv, tzs, ty, txp, txm, final,
-           u, rhs, permb, poreb, ysend, yrecv, xsend, xrecv,
+           u, rhs, permb, poreb, ysend, yrecv, xsend, xrecv, zrecv, yedge, rowk,
            flux, tot, zplanes, ext, cxsend, cxrecv, field,
            in_sem, h_send, h_recv, z_send, z_recv, c_send, c_recv):
     ngx, ngy, ngz, nz, ny, nx = sizes
@@ -64,8 +64,8 @@
         ref[...] = jnp.zeros(ref.shape, ref.dtype)
 
     for cond, refs in (
-        (iz == 0, [u.at[:, 0, own]]),
-        (iz == ngz - 1, [u.at[:, nz + 1, own]]),
+        (iz == 0, [zrecv.at[0]]),
+        (iz == ngz - 1, [zrecv.at[1]]),
         (iy == 0, [yrecv.at[0], ext.at[:, 0:HALO]]),
         (iy == ngy - 1, [yrecv.at[1], ext.at[:, HALO + ny:]]),
         (ix == 0, [xrecv.at[0], cxrecv.at[0, own]]),
@@ -80,27 +80,40 @@
             for ref in refs:
                 zero(ref)
     zero(field)
+    zero(u.at[:, nz + 1, own])
+    zero(u.at[:, 0, own])
 
     loads[0].wait()
+
+    def loop(begin, end, body, carry, unroll):
+        def several(i, carry):
+            for k in range(unroll):
+                carry = body(begin + i * unroll + k, carry)
+            return carry
+        return lax.fori_loop(0, (end - begin) // unroll, several, carry)
+
+    def coefficient(table, z, r, c):
+        return table[r, facies[z], c]
 
     def widen(z, _):
         u[3, z + 1, own, :] = permb[z].astype(jnp.float32)
+        for k in range(4):
+            u[k, z + 1, 0:HALO, :] = jnp.zeros((HALO, nx), jnp.float32)
+            u[k, z + 1, HALO + ny:, :] = jnp.zeros((HALO, nx), jnp.float32)
+            rowk[pl.ds(k * nz + z, 1), :] = jnp.full((1, nx), coefficient(ktab, z, 0, k % 3), jnp.float32)
         return 0
 
-    lax.fori_loop(0, nz, widen, 0)
+    loop(0, nz, widen, 0, 2)
     loads[1].wait()
 
-    def pack(z, packed):
+    def pack_rows(z, _):
         for k in range(4):
-            slab = u[k, z + 1, own, :]
             j = k * nz + z
             ysend[0, pl.ds(j, 1), :] = u[k, z + 1, HALO:HALO + 1, :]
             ysend[1, pl.ds(j, 1), :] = u[k, z + 1, HALO + ny - 1:HALO + ny, :]
-            packed = jnp.where(lax.shift_right_logical(lane, 1) == j,
-                               pltpu.roll(slab, lax.rem(2 * j + 1, nx), 1), packed)
-        return packed
-
-    xsend[...] = lax.fori_loop(0, nz, pack, jnp.zeros((ny, nx), jnp.float32))
+        return 0
+
+    loop(0, nz, pack_rows, 0, 4)
 
     count = sum(exists(*side).astype(jnp.int32) for side in SIDES) + (ngz - 1)
     pl.semaphore_wait(barrier, count)
@@ -113,8 +126,8 @@
         return {"gx": ix, "gy": iy, "gz": iz + d}
 
     halos = [
-        (iz < ngz - 1, iz > 0, remote(u.at[:, nz, own], u.at[:, 0, own], h_send.at[0], h_recv.at[0], z_device(1))),
-        (iz > 0, iz < ngz - 1, remote(u.at[:, 1, own], u.at[:, nz + 1, own], h_send.at[1], h_recv.at[1], z_device(-1))),
+        (iz < ngz - 1, iz > 0, remote(u.at[:, nz, own], zrecv.at[0], h_send.at[0], h_recv.at[0], z_device(1))),
+        (iz > 0, iz < ngz - 1, remote(u.at[:, 1, own], zrecv.at[1], h_send.at[1], h_recv.at[1], z_device(-1))),
         (exists(1, 0), exists(-1, 0), remote(ysend.at[1], yrecv.at[0], h_send.at[2], h_recv.at[2], at(1, 0))),
         (exists(-1, 0), exists(1, 0), remote(ysend.at[0], yrecv.at[1], h_send.at[3], h_recv.at[3], at(-1, 0))),
         (exists(0, 1), exists(0, -1), remote(xsend, xrecv.at[0], h_send.at[4], h_recv.at[4], at(0, 1))),
@@ -139,44 +152,38 @@
             def _(copy=copy):
                 copy.wait_send()
 
+    start(halos[:4])
+
+    lane_row = lane[0:1]
+
+    def pack_columns(z, carry):
+        packed, lanek = carry
+        for k in range(4):
+            j = k * nz + z
+            packed = jnp.where(lax.shift_right_logical(lane, 1) == j,
+                               pltpu.roll(u[k, z + 1, own, :], lax.rem(2 * j + 1, nx), 1), packed)
+            lanek = jnp.where(lax.shift_right_logical(lane_row, 1) == j, coefficient(ktab, z, 0, k % 3), lanek)
+        return packed, lanek
+
+    nil = jnp.zeros((ny, nx), jnp.float32)
+    packed, lanek = loop(0, nz, pack_columns, (nil, jnp.zeros((1, nx), jnp.float32)), 4)
+    xsend[...] = packed
     start(halos[4:])
-    start(halos[2:4])
-    start(halos[:2])
     loads[2].wait()
     loads[3].wait()
-    wait_recv(halos)
-
-    left = xrecv[0]
-    border = jnp.where(lax.rem(lane, 2) == 0, left, pltpu.roll(xrecv[1], nx - 2, 1))
-    mine = pltpu.roll(xsend[...], nx - 1, 1)
-    left_t = jnp.where(lane >= 6 * nz, face(jnp.where(lane >= 6 * nz, left, 1.0), jnp.where(lane >= 6 * nz, mine, 1.0)), 0.0)
+
     first, last = lane == 0, lane == nx - 1
-
-    def coefficient(table, z, r, c):
-        return table[r, facies[z], c]
 
     def assemble(z, carry):
         tzm, s_rhs, s_diag, s_ty, s_tx = carry
-        for k in range(4):
-            j = k * nz + z
-            u[k, z + 1, HALO - 1:HALO, :] = yrecv[0, pl.ds(j, 1), :]
-            u[k, z + 1, HALO + ny:HALO + ny + 1, :] = yrecv[1, pl.ds(j, 1), :]
-
-        def around(k):
-            c = u[k, z + 1, own, :]
-            h = pltpu.roll(border, lax.rem(2 * nx - 2 * (k * nz + z), nx), 1)
-            return (c, u[k, z + 2, own, :], u[k, z, own, :],
-                    u[k, z + 1, HALO + 1:HALO + ny + 1, :], u[k, z + 1, HALO - 1:HALO + ny - 1, :],
-                    jnp.where(last, h, pltpu.roll(c, nx - 1, 1)), jnp.where(first, h, pltpu.roll(c, 1, 1)))
-
-        q, qzp, _, qyp, _, qxp, _ = around(3)
-        tzp = face(q, qzp)
-        typ = face(q, qyp)
+        q = u[3, z + 1, own, :]
+        tzp = face(q, u[3, z + 2, own, :])
+        typ = face(q, u[3, z + 1, HALO + 1:HALO + ny + 1, :])
         ty[z, own, :] = typ
-        ty[z, HALO - 1:HALO, :] = face(u[3, z + 1, HALO - 1:HALO, :], u[3, z + 1, HALO:HALO + 1, :])
+        ty[z, 0:HALO, :] = jnp.zeros((HALO, nx), jnp.float32)
         tym = ty[z, HALO - 1:HALO + ny - 1, :]
-        xp = face(q, qxp)
-        xm = jnp.where(first, pltpu.roll(left_t, lax.rem(2 * nx - 2 * (3 * nz + z), nx), 1), pltpu.roll(xp, 1, 1))
+        xp = jnp.where(last, 0.0, face(q, pltpu.roll(q, nx - 1, 1)))
+        xm = pltpu.roll(xp, 1, 1)
         txp[z] = xp
         txm[z] = xm
         tz = tzp + tzm
@@ -186,22 +193,69 @@
         v = poreb[z].astype(jnp.float32)
         local, moved = 0.0, 0.0
         for k in range(3):
-            c, zp, zm, yp, ym, cxp, cxm = around(k)
-            f = (tzp * (c - zp) + tzm * (c - zm) + typ * (c - yp) + tym * (c - ym)
-                 + xp * (c - cxp) + xm * (c - cxm))
+            c = u[k, z + 1, own, :]
+            f = (tzp * (c - u[k, z + 2, own, :]) + tzm * (c - u[k, z, own, :])
+                 + typ * (c - u[k, z + 1, HALO + 1:HALO + ny + 1, :])
+                 + tym * (c - u[k, z + 1, HALO - 1:HALO + ny - 1, :])
+                 + xp * (c - pltpu.roll(c, nx - 1, 1)) + xm * (c - pltpu.roll(c, 1, 1)))
             flux[k, z] = f
             local = local + coefficient(mtab, z, 0, k) * c
             moved = moved + coefficient(ktab, z, 0, k) * f
         res = rhs[0, z] - (v * local + moved)
-        rhs[0, z] = res
         k00 = coefficient(ktab, z, 0, 0)
         return (tzp, s_rhs + res, s_diag + (v * coefficient(mtab, z, 0, 0) + k00 * areal),
                 s_ty + k00 * typ, s_tx + k00 * xp)
 
-    nil = jnp.zeros((ny, nx), jnp.float32)
-    carry = lax.fori_loop(0, nz, assemble, (face(u[3, 1, own, :], u[3, 0, own, :]), nil, nil, nil, nil))
-    for p in range(PLANES):
-        zplanes[iz, p] = carry[p + 1]
+    _, s_rhs, s_diag, s_ty, s_tx = loop(0, nz, assemble, (nil,) * 5, 2)
+    wait_recv(halos)
+
+    for side, z in ((0, 0), (1, nz - 1)):
+        t = face(u[3, z + 1, own, :], zrecv[side, 3])
+        for k in range(3):
+            f = t * (u[k, z + 1, own, :] - zrecv[side, k])
+            flux[k, z] = flux[k, z] + f
+            s_rhs = s_rhs - coefficient(ktab, z, 0, k) * f
+        tzs[z] = tzs[z] + t
+        tot[z] = tot[z] + t
+
+    row = lax.broadcasted_iota(jnp.int32, (ny, nx), 0)
+    for side, at_row in ((0, 0), (1, ny - 1)):
+        t = face(ysend[side, 3 * nz:, :], yrecv[side, 3 * nz:, :])
+        f = [t * (ysend[side, k * nz:(k + 1) * nz, :] - yrecv[side, k * nz:(k + 1) * nz, :]) for k in range(3)]
+        for k, x in enumerate(f + [t]):
+            yedge[side, k * nz:(k + 1) * nz, :] = x
+        moved = sum(rowk[k * nz:(k + 1) * nz, :] * f[k] for k in range(3))
+        moved = jnp.sum(moved, axis=0, keepdims=True)
+        weight = jnp.sum(rowk[3 * nz:, :] * t, axis=0, keepdims=True)
+        here = row == at_row
+        s_rhs = s_rhs - jnp.where(here, moved, 0.0)
+        s_diag = s_diag + jnp.where(here, weight, 0.0)
+        if side:
+            s_ty = s_ty + jnp.where(here, weight, 0.0)
+
+    even = lax.rem(lane, 2) == 0
+    weights_at = jnp.logical_and(even, lane >= 6 * nz)
+    fluxes_at = jnp.logical_and(even, lane < 6 * nz)
+    edges = []
+    for side, edge in ((0, first), (1, last)):
+        if side:
+            here, there = xsend[...], pltpu.roll(xrecv[1], nx - 1, 1)
+        else:
+            here, there = pltpu.roll(xsend[...], nx - 1, 1), xrecv[0]
+        t = jnp.where(weights_at, face(jnp.where(weights_at, here, 1.0), jnp.where(weights_at, there, 1.0)), 0.0)
+        every = sum(pltpu.roll(t, nx - 2 * (3 - k) * nz, 1) for k in range(3))
+        f = jnp.where(fluxes_at, every * (here - there), 0.0)
+        moved = jnp.sum(f * lanek, axis=1, keepdims=True)
+        weight = jnp.sum(t * lanek, axis=1, keepdims=True)
+        s_rhs = s_rhs - jnp.where(edge, moved, 0.0)
+        s_diag = s_diag + jnp.where(edge, weight, 0.0)
+        if side:
+            s_tx = s_tx + jnp.where(edge, weight, 0.0)
+        edges.append(f + t)
+    border = jnp.where(even, edges[0], pltpu.roll(edges[1], nx - 1, 1))
+
+    for p, plane in enumerate((s_rhs, s_diag, s_ty, s_tx)):
+        zplanes[iz, p] = plane
 
     others = [lax.rem(iz + d, ngz) for d in range(1, ngz)]
     sums = [remote(zplanes.at[iz], zplanes.at[iz], z_send.at[d], z_recv.at[iz], {"gx": ix, "gy": iy, "gz": peer})
@@ -209,9 +263,27 @@
     for copy in sums:
         copy.start()
 
+    outer = jnp.logical_or(first, last)
+
     def solve(z, _):
         v = poreb[z].astype(jnp.float32)
-        total = tot[z]
+        for side, at_row in ((0, 0), (1, ny - 1)):
+            here = slice(at_row, at_row + 1)
+            for k in range(3):
+                flux[k, z, here, :] = flux[k, z, here, :] + yedge[side, pl.ds(k * nz + z, 1), :]
+            t = yedge[side, pl.ds(3 * nz + z, 1), :]
+            tot[z, here, :] = tot[z, here, :] + t
+            at_face = HALO - 1 + side * ny
+            ty[z, at_face:at_face + 1, :] = t
+
+        def beside(k):
+            shifted = pltpu.roll(border, lax.rem(2 * nx - 2 * (k * nz + z), nx), 1)
+            return jnp.where(outer, shifted, 0.0)
+
+        t = beside(3)
+        txp[z] = txp[z] + jnp.where(last, t, 0.0)
+        txm[z] = txm[z] + jnp.where(first, t, 0.0)
+        total = tot[z] + t
         m = [[coefficient(mtab, z, r, c) for c in range(3)] for r in range(3)]
         kk = [[coefficient(ktab, z, r, c) for c in range(3)] for r in range(3)]
         e = [[v * m[r][c] + total * kk[r][c] for c in range(3)] for r in range(3)]
@@ -221,9 +293,9 @@
                     - e[(r + 1) % 3][(c + 2) % 3] * e[(r + 2) % 3][(c + 1) % 3])
 
         cells = [u[k, z + 1, own, :] for k in range(3)]
-        f = [flux[k, z] for k in range(3)]
-        res = [rhs[0, z]]
-        for r in (1, 2):
+        f = [flux[k, z] + beside(k) for k in range(3)]
+        res = []
+        for r in range(3):
             res.append(rhs[r, z] - (v * (m[r][0] * cells[0] + m[r][1] * cells[1] + m[r][2] * cells[2])
                                     + (kk[r][0] * f[0] + kk[r][1] * f[1] + kk[r][2] * f[2])))
         fac = [[cofactor(r, c) for c in range(3)] for r in range(3)]
@@ -234,7 +306,7 @@
         return 0
 
     half = nz // 4
-    lax.fori_loop(0, half, solve, 0)
+    loop(0, half, solve, 0, 2)
 
     for peer in others:
         remote(zplanes.at[peer], zplanes.at[peer], z_send.at[0], z_recv.at[peer],
@@ -262,7 +334,7 @@
             src, dst = cxsend.at[rows], cxrecv.at[0 if dx > 0 else 1, into]
         coarse.append((exists(dy, dx), exists(-dy, -dx), remote(src, dst, c_send.at[s], c_recv.at[s], at(dy, dx))))
     start(coarse)
-    lax.fori_loop(half, nz, solve, 0)
+    loop(half, nz, solve, 0, 2)
     wait_recv(coarse)
 
     rows = ny + 2 * HALO
@@ -362,6 +434,7 @@
             vmem(4, nz + 2, ey, nx), vmem(3, *cells),
             pltpu.VMEM(cells, permeability.dtype), pltpu.VMEM(cells, pore_volume.dtype),
             vmem(2, 4 * nz, nx), vmem(2, 4 * nz, nx), vmem(ny, nx), vmem(2, ny, nx),
+            vmem(2, 4, ny, nx), vmem(2, 4 * nz, nx), vmem(4 * nz, nx),
             vmem(3, *cells), vmem(*cells),
             vmem(ngz, PLANES, ny, nx), vmem(PLANES, ey, nx),
             vmem(ny, nx), vmem(2, ey, nx), vmem(2, ey + 2 * HALO, nx),

time: 19.9 us -> 18 us (0.905)
  Pallas kernels: 19.1 us -> 17.2 us
    pallas_call x1, Pallas kernels: 17.4 us -> 15.5 us  [per_device(): pl.pallas_call(functools.partial(kernel, sizes), out_shape=(vmem(3, *cell...]
where the time goes in v3:
time: 18 us; the launch traced here: 17.8 us
  Pallas kernels  17.2 us (96%)
  between operations  0.64 us (4%)
    pallas_call x1, Pallas kernels, per_device(): pl.pallas_call(functools.partial(kernel, sizes), out_shape=(vmem(3, *cell...  15.5 us
    pallas_call x1, Pallas kernels, per_device(): pl.pallas_call(functools.partial(finish_kernel, parts), out_shape=(jax.Sh...  1.65 us

profile of v3, /device:TPU:0, one launch (start us, length us, event | category | flops | bytes accessed | tf_op | source)
XLA Modules:
  0.0 17.8 jit_solution(447625209365880350)
XLA Ops:
  0.6 15.5 %cpr_apply.1 = (f32[3,16,40,128]{3,2,1,0:T(8,128)S(1)}, f32[3,16,40,128]{3,2,1,0:T(8,128)S(1)}, f32[16,40,128]{2,1,0:T(8,128)S(1)}, f32[16,56,128]{2,1,0:T(8,128...) custom-call(s32[16]{0:T(128)} %facies.1, f32[3,4,3]{2,1,0:T(4,128)} %bitcast.2, ...), custom_call_target="tpu_custom_call" | custom-call | tf_op jit(solution)/shard_map/cpr_apply/pallas_call | solution.py:427
  16.2 1.6 %cpr_finish.1 = (f32[3,16,40,128]{3,2,1,0:T(8,128)}, f32[40,128]{1,0:T(8,128)}) custom-call(f32[3,16,40,128]{3,2,1,0:T(8,128)S(1)} %get-tuple-element.9.w, f32[3,16,40,128]{3,2,1,0:T(8,128)S(1)} %get-tuple-element.10.qv, f32[16,40,128]{2,1,0:T(8,128)S(1)} %get-tuple-element.11.tzs, f32[16,56,128]{2,1,0:T(8,128)S(1)} %get-tuple-element.12.ty, ...), custom_call_target="tpu_custom_call" | custom-call | tf_op jit(solution)/shard_map/cpr_finish/pallas_call | solution.py:448

commit v4 on v3

--- a/solution.py
+++ b/solution.py
@@ -20,23 +20,14 @@
     return 2.0 * a * b / (a + b)
 
 
-def kernel(sizes, facies, mtab, ktab, state_hbm, rhs_hbm, perm_hbm, pore_hbm,
+def kernel(sizes, facies_hbm, mtab_hbm, ktab_hbm, state_hbm, rhs_hbm, perm_hbm, pore_hbm,
            w, qv, tzs, ty, txp, txm, final,
            u, rhs, permb, poreb, ysend, yrecv, xsend, xrecv, zrecv, yedge, rowk,
            flux, tot, zplanes, ext, cxsend, cxrecv, field,
-           in_sem, h_send, h_recv, z_send, z_recv, c_send, c_recv):
+           facies, mtab, ktab, near_sem, in_sem, h_send, h_recv, z_send, z_recv, c_send, c_recv):
     ngx, ngy, ngz, nz, ny, nx = sizes
     ix, iy, iz = lax.axis_index("gx"), lax.axis_index("gy"), lax.axis_index("gz")
     own = slice(HALO, HALO + ny)
-
-    loads = [
-        pltpu.make_async_copy(perm_hbm, permb, in_sem.at[0]),
-        pltpu.make_async_copy(state_hbm, u.at[0:3, 1:nz + 1, own], in_sem.at[1]),
-        pltpu.make_async_copy(pore_hbm, poreb, in_sem.at[2]),
-        pltpu.make_async_copy(rhs_hbm, rhs, in_sem.at[3]),
-    ]
-    for load in loads:
-        load.start()
 
     def exists(dy, dx):
         ok = None
@@ -50,13 +41,25 @@
         return {"gx": ix + dx, "gy": iy + dy, "gz": iz}
 
     barrier = pltpu.get_barrier_semaphore()
-    for side in SIDES:
+    for side in SIDES[:4]:
         @pl.when(exists(*side))
         def _(side=side):
             pl.semaphore_signal(barrier, inc=1, device_id=at(*side), device_id_type=MESH)
     for d in range(1, ngz):
         pl.semaphore_signal(barrier, inc=1, device_id={"gx": ix, "gy": iy, "gz": lax.rem(iz + d, ngz)},
                             device_id_type=MESH)
+
+    loads = [
+        pltpu.make_async_copy(perm_hbm, permb, in_sem.at[0]),
+        pltpu.make_async_copy(state_hbm, u.at[0:3, 1:nz + 1, own], in_sem.at[1]),
+        pltpu.make_async_copy(pore_hbm, poreb, in_sem.at[2]),
+        pltpu.make_async_copy(rhs_hbm, rhs, in_sem.at[3]),
+        pltpu.make_async_copy(facies_hbm, facies, in_sem.at[4]),
+        pltpu.make_async_copy(mtab_hbm, mtab, in_sem.at[5]),
+        pltpu.make_async_copy(ktab_hbm, ktab, in_sem.at[6]),
+    ]
+    for load in loads:
+        load.start()
 
     lane = lax.broadcasted_iota(jnp.int32, (ny, nx), 1)
 
@@ -84,6 +87,8 @@
     zero(u.at[:, 0, own])
 
     loads[0].wait()
+    for load in loads[4:]:
+        load.wait()
 
     def loop(begin, end, body, carry, unroll):
         def several(i, carry):
@@ -115,8 +120,12 @@
 
     loop(0, nz, pack_rows, 0, 4)
 
-    count = sum(exists(*side).astype(jnp.int32) for side in SIDES) + (ngz - 1)
-    pl.semaphore_wait(barrier, count)
+    count = sum(exists(*side).astype(jnp.int32) for side in SIDES[:4])
+    pl.semaphore_wait(barrier, count + (ngz - 1))
+    for side in SIDES[:4]:
+        @pl.when(exists(*side))
+        def _(side=side):
+            pl.semaphore_signal(near_sem, inc=1, device_id=at(*side), device_id_type=MESH)
 
     def remote(src, dst, send, recv, device):
         return pltpu.make_async_remote_copy(src_ref=src, dst_ref=dst, send_sem=send, recv_sem=recv,
@@ -333,6 +342,7 @@
         else:
             src, dst = cxsend.at[rows], cxrecv.at[0 if dx > 0 else 1, into]
         coarse.append((exists(dy, dx), exists(-dy, -dx), remote(src, dst, c_send.at[s], c_recv.at[s], at(dy, dx))))
+    pl.semaphore_wait(near_sem, count)
     start(coarse)
     loop(half, nz, solve, 0, 2)
     wait_recv(coarse)
@@ -418,9 +428,9 @@
     cells = (nz, ny, nx)
     vmem = lambda *shape: pltpu.VMEM(shape, f32)
     hbm = pl.BlockSpec(memory_space=pltpu.HBM)
-    smem = pl.BlockSpec(memory_space=pltpu.SMEM)
     dma = lambda n: pltpu.SemaphoreType.DMA((n,))
     ey = ny + 2 * HALO
+    facets = storage_table.shape[0]
     in_vmem = pl.BlockSpec(memory_space=pltpu.VMEM)
     handed = 4 * nx * (9 * nz * ny + nz * ey + 3 * ey)
     limit = 16384 * ((VMEM_BYTES - handed) // 16384)
@@ -428,7 +438,7 @@
         functools.partial(kernel, sizes),
         out_shape=(vmem(3, *cells), vmem(3, *cells), vmem(*cells), vmem(nz, ey, nx), vmem(*cells), vmem(*cells),
                    vmem(3, ey, nx)),
-        in_specs=[smem, smem, smem, hbm, hbm, hbm, hbm],
+        in_specs=[hbm, hbm, hbm, hbm, hbm, hbm, hbm],
         out_specs=(in_vmem,) * 7,
         scratch_shapes=[
             vmem(4, nz + 2, ey, nx), vmem(3, *cells),
@@ -438,7 +448,8 @@
             vmem(3, *cells), vmem(*cells),
             vmem(ngz, PLANES, ny, nx), vmem(PLANES, ey, nx),
             vmem(ny, nx), vmem(2, ey, nx), vmem(2, ey + 2 * HALO, nx),
-            dma(4), dma(6), dma(6), dma(max(ngz - 1, 1)), dma(ngz), dma(8), dma(8),
+            pltpu.SMEM((nz,), facies.dtype), pltpu.SMEM((3, facets, 3), f32), pltpu.SMEM((3, facets, 3), f32),
+            pltpu.SemaphoreType.REGULAR, dma(7), dma(6), dma(6), dma(max(ngz - 1, 1)), dma(ngz), dma(8), dma(8),
         ],
         compiler_params=pltpu.CompilerParams(collective_id=0, has_side_effects=True, vmem_limit_bytes=limit),
         name="cpr_apply",

time: 18 us -> 16.2 us (0.90)
  Pallas kernels: 17.2 us -> 15.4 us
    pallas_call x1, Pallas kernels: 15.5 us -> 13.7 us  [per_device(): pl.pallas_call(functools.partial(kernel, sizes), out_shape=(vmem(3, *cell...]
where the time goes in v4:
time: 16.2 us; the launch traced here: 16 us
  Pallas kernels  15.4 us (95%)
  between operations  0.64 us (4%)
    pallas_call x1, Pallas kernels, per_device(): pl.pallas_call(functools.partial(kernel, sizes), out_shape=(vmem(3, *cell...  13.7 us
    pallas_call x1, Pallas kernels, per_device(): pl.pallas_call(functools.partial(finish_kernel, parts), out_shape=(jax.Sh...  1.65 us

profile of v4, /device:TPU:0, one launch (start us, length us, event | category | flops | bytes accessed | tf_op | source)
XLA Modules:
  0.0 16.0 jit_solution(13867340674418948390)
XLA Ops:
  0.6 13.7 %cpr_apply.1 = (f32[3,16,40,128]{3,2,1,0:T(8,128)S(1)}, f32[3,16,40,128]{3,2,1,0:T(8,128)S(1)}, f32[16,40,128]{2,1,0:T(8,128)S(1)}, f32[16,56,128]{2,1,0:T(8,128...) custom-call(s32[16]{0:T(128)} %facies_hbm.1, f32[3,4,3]{2,1,0:T(4,128)} %bitcast.2, ...), custom_call_target="tpu_custom_call" | custom-call | tf_op jit(solution)/shard_map/cpr_apply/pallas_call | solution.py:437
  14.4 1.6 %cpr_finish.1 = (f32[3,16,40,128]{3,2,1,0:T(8,128)}, f32[40,128]{1,0:T(8,128)}) custom-call(f32[3,16,40,128]{3,2,1,0:T(8,128)S(1)} %get-tuple-element.9.w, f32[3,16,40,128]{3,2,1,0:T(8,128)S(1)} %get-tuple-element.10.qv, f32[16,40,128]{2,1,0:T(8,128)S(1)} %get-tuple-element.11.tzs, f32[16,56,128]{2,1,0:T(8,128)S(1)} %get-tuple-element.12.ty, ...), custom_call_target="tpu_custom_call" | custom-call | tf_op jit(solution)/shard_map/cpr_finish/pallas_call | solution.py:459

commit v5 on v4

--- a/solution.py
+++ b/solution.py
@@ -18,6 +18,10 @@
 
 def face(a, b):
     return 2.0 * a * b / (a + b)
+
+
+def upper_rows(ny):
+    return HALO * (-(-ny // (2 * HALO)))
 
 
 def kernel(sizes, facies_hbm, mtab_hbm, ktab_hbm, state_hbm, rhs_hbm, perm_hbm, pore_hbm,
@@ -28,6 +32,7 @@
     ngx, ngy, ngz, nz, ny, nx = sizes
     ix, iy, iz = lax.axis_index("gx"), lax.axis_index("gy"), lax.axis_index("gz")
     own = slice(HALO, HALO + ny)
+    split = upper_rows(ny)
 
     def exists(dy, dx):
         ok = None
@@ -69,10 +74,10 @@
     for cond, refs in (
         (iz == 0, [zrecv.at[0]]),
         (iz == ngz - 1, [zrecv.at[1]]),
-        (iy == 0, [yrecv.at[0], ext.at[:, 0:HALO]]),
-        (iy == ngy - 1, [yrecv.at[1], ext.at[:, HALO + ny:]]),
-        (ix == 0, [xrecv.at[0], cxrecv.at[0, own]]),
-        (ix == ngx - 1, [xrecv.at[1], cxrecv.at[1, own]]),
+        (iy == 0, [yrecv.at[:, 0], ext.at[:, 0:HALO]]),
+        (iy == ngy - 1, [yrecv.at[:, 1], ext.at[:, HALO + ny:]]),
+        (ix == 0, [xrecv.at[:, 0], cxrecv.at[0, own]]),
+        (ix == ngx - 1, [xrecv.at[:, 1], cxrecv.at[1, own]]),
         (jnp.logical_or(iy == 0, ix == 0), [cxrecv.at[0, 0:HALO]]),
         (jnp.logical_or(iy == 0, ix == ngx - 1), [cxrecv.at[1, 0:HALO]]),
         (jnp.logical_or(iy == ngy - 1, ix == 0), [cxrecv.at[0, HALO + ny:]]),
@@ -105,20 +110,27 @@
         for k in range(4):
             u[k, z + 1, 0:HALO, :] = jnp.zeros((HALO, nx), jnp.float32)
             u[k, z + 1, HALO + ny:, :] = jnp.zeros((HALO, nx), jnp.float32)
-            rowk[pl.ds(k * nz + z, 1), :] = jnp.full((1, nx), coefficient(ktab, z, 0, k % 3), jnp.float32)
+        rowk[pl.ds(z, 1), :] = jnp.full((1, nx), coefficient(ktab, z, 0, 0), jnp.float32)
         return 0
 
     loop(0, nz, widen, 0, 2)
     loads[1].wait()
 
-    def pack_rows(z, _):
-        for k in range(4):
-            j = k * nz + z
-            ysend[0, pl.ds(j, 1), :] = u[k, z + 1, HALO:HALO + 1, :]
-            ysend[1, pl.ds(j, 1), :] = u[k, z + 1, HALO + ny - 1:HALO + ny, :]
-        return 0
-
-    loop(0, nz, pack_rows, 0, 4)
+    def pair(batch, z, part):
+        if batch:
+            return part(1), part(2)
+        return sum(coefficient(ktab, z, 0, k) * part(k) for k in range(3)), part(3)
+
+    def pack_rows(batch):
+        def body(z, _):
+            for side, at_row in ((0, HALO), (1, HALO + ny - 1)):
+                for i, x in enumerate(pair(batch, z, lambda k: u[k, z + 1, at_row:at_row + 1, :])):
+                    ysend[batch, side, pl.ds(i * nz + z, 1), :] = x
+            return 0
+
+        loop(0, nz, body, 0, 4)
+
+    pack_rows(0)
 
     count = sum(exists(*side).astype(jnp.int32) for side in SIDES[:4])
     pl.semaphore_wait(barrier, count + (ngz - 1))
@@ -137,10 +149,16 @@
     halos = [
         (iz < ngz - 1, iz > 0, remote(u.at[:, nz, own], zrecv.at[0], h_send.at[0], h_recv.at[0], z_device(1))),
         (iz > 0, iz < ngz - 1, remote(u.at[:, 1, own], zrecv.at[1], h_send.at[1], h_recv.at[1], z_device(-1))),
-        (exists(1, 0), exists(-1, 0), remote(ysend.at[1], yrecv.at[0], h_send.at[2], h_recv.at[2], at(1, 0))),
-        (exists(-1, 0), exists(1, 0), remote(ysend.at[0], yrecv.at[1], h_send.at[3], h_recv.at[3], at(-1, 0))),
-        (exists(0, 1), exists(0, -1), remote(xsend, xrecv.at[0], h_send.at[4], h_recv.at[4], at(0, 1))),
-        (exists(0, -1), exists(0, 1), remote(xsend, xrecv.at[1], h_send.at[5], h_recv.at[5], at(0, -1))),
+        (exists(1, 0), exists(-1, 0), remote(ysend.at[0, 1], yrecv.at[0, 0], h_send.at[2], h_recv.at[2], at(1, 0))),
+        (exists(-1, 0), exists(1, 0), remote(ysend.at[0, 0], yrecv.at[0, 1], h_send.at[3], h_recv.at[3], at(-1, 0))),
+        (exists(0, 1), exists(0, -1), remote(xsend.at[0], xrecv.at[0, 0], h_send.at[4], h_recv.at[4], at(0, 1))),
+        (exists(0, -1), exists(0, 1), remote(xsend.at[0], xrecv.at[0, 1], h_send.at[5], h_recv.at[5], at(0, -1))),
+    ]
+    rest = [
+        (exists(1, 0), exists(-1, 0), remote(ysend.at[1, 1], yrecv.at[1, 0], h_send.at[6], h_recv.at[6], at(1, 0))),
+        (exists(-1, 0), exists(1, 0), remote(ysend.at[1, 0], yrecv.at[1, 1], h_send.at[7], h_recv.at[7], at(-1, 0))),
+        (exists(0, 1), exists(0, -1), remote(xsend.at[1], xrecv.at[1, 0], h_send.at[8], h_recv.at[8], at(0, 1))),
+        (exists(0, -1), exists(0, 1), remote(xsend.at[1], xrecv.at[1, 1], h_send.at[9], h_recv.at[9], at(0, -1))),
     ]
 
     def start(copies):
@@ -163,21 +181,35 @@
 
     start(halos[:4])
 
-    lane_row = lane[0:1]
-
-    def pack_columns(z, carry):
-        packed, lanek = carry
-        for k in range(4):
-            j = k * nz + z
-            packed = jnp.where(lax.shift_right_logical(lane, 1) == j,
-                               pltpu.roll(u[k, z + 1, own, :], lax.rem(2 * j + 1, nx), 1), packed)
-            lanek = jnp.where(lax.shift_right_logical(lane_row, 1) == j, coefficient(ktab, z, 0, k % 3), lanek)
-        return packed, lanek
-
+    half = nx // 2
+    lane_pair = lax.shift_right_logical(lane, 1)
     nil = jnp.zeros((ny, nx), jnp.float32)
-    packed, lanek = loop(0, nz, pack_columns, (nil, jnp.zeros((1, nx), jnp.float32)), 4)
-    xsend[...] = packed
+
+    def pack_columns(batch):
+        def body(z, carry):
+            packed, lanek = carry
+            for i, x in enumerate(pair(batch, z, lambda k: u[k, z + 1, own, :])):
+                j = i * nz + z
+                upper = pltpu.roll(x[:split], 2 * j + 1, 1)
+                lower = pltpu.roll(x[split:], lax.rem(2 * j + 1 + half, nx), 1)
+                packed = jnp.where(lane_pair[:split] == j, upper, packed)
+                beside = jnp.where(lane_pair[:ny - split] == j + half // 2, lower, packed[:ny - split])
+                packed = beside if ny == 2 * split else jnp.concatenate([beside, packed[ny - split:]], axis=0)
+            lanek = jnp.where(lane_pair[0:1] == nz + z, coefficient(ktab, z, 0, 0), lanek)
+            return packed, lanek
+
+        packed, lanek = loop(0, nz, body, (nil[:split], nil[0:1]), 4)
+        xsend[batch] = packed
+        return lanek
+
+    def unpacked(x):
+        return jnp.concatenate([x, pltpu.roll(x[:ny - split], half, 1)], axis=0)
+
+    lanek = pack_columns(0)
     start(halos[4:])
+    pack_rows(1)
+    pack_columns(1)
+    start(rest)
     loads[2].wait()
     loads[3].wait()
 
@@ -229,13 +261,12 @@
 
     row = lax.broadcasted_iota(jnp.int32, (ny, nx), 0)
     for side, at_row in ((0, 0), (1, ny - 1)):
-        t = face(ysend[side, 3 * nz:, :], yrecv[side, 3 * nz:, :])
-        f = [t * (ysend[side, k * nz:(k + 1) * nz, :] - yrecv[side, k * nz:(k + 1) * nz, :]) for k in range(3)]
-        for k, x in enumerate(f + [t]):
-            yedge[side, k * nz:(k + 1) * nz, :] = x
-        moved = sum(rowk[k * nz:(k + 1) * nz, :] * f[k] for k in range(3))
-        moved = jnp.sum(moved, axis=0, keepdims=True)
-        weight = jnp.sum(rowk[3 * nz:, :] * t, axis=0, keepdims=True)
+        t = face(ysend[0, side, nz:, :], yrecv[0, side, nz:, :])
+        f = t * (ysend[0, side, :nz, :] - yrecv[0, side, :nz, :])
+        yedge[side, 0:nz, :] = f
+        yedge[side, 3 * nz:, :] = t
+        moved = jnp.sum(f, axis=0, keepdims=True)
+        weight = jnp.sum(rowk[...] * t, axis=0, keepdims=True)
         here = row == at_row
         s_rhs = s_rhs - jnp.where(here, moved, 0.0)
         s_diag = s_diag + jnp.where(here, weight, 0.0)
@@ -243,25 +274,33 @@
             s_ty = s_ty + jnp.where(here, weight, 0.0)
 
     even = lax.rem(lane, 2) == 0
-    weights_at = jnp.logical_and(even, lane >= 6 * nz)
-    fluxes_at = jnp.logical_and(even, lane < 6 * nz)
-    edges = []
+    low_at = jnp.logical_and(even, lane < 2 * nz)
+    high_at = jnp.logical_and(even, jnp.logical_and(lane >= 2 * nz, lane < 4 * nz))
+
+    def columns(batch, side):
+        mine, other = unpacked(xsend[batch]), unpacked(xrecv[batch, side])
+        if side:
+            return mine, pltpu.roll(other, nx - 1, 1)
+        return pltpu.roll(mine, nx - 1, 1), other
+
+    def merged(edges):
+        return jnp.where(even, edges[0], pltpu.roll(edges[1], nx - 1, 1))
+
+    edges, spread = [], []
     for side, edge in ((0, first), (1, last)):
-        if side:
-            here, there = xsend[...], pltpu.roll(xrecv[1], nx - 1, 1)
-        else:
-            here, there = pltpu.roll(xsend[...], nx - 1, 1), xrecv[0]
-        t = jnp.where(weights_at, face(jnp.where(weights_at, here, 1.0), jnp.where(weights_at, there, 1.0)), 0.0)
-        every = sum(pltpu.roll(t, nx - 2 * (3 - k) * nz, 1) for k in range(3))
-        f = jnp.where(fluxes_at, every * (here - there), 0.0)
-        moved = jnp.sum(f * lanek, axis=1, keepdims=True)
+        here, there = columns(0, side)
+        t = jnp.where(high_at, face(jnp.where(high_at, here, 1.0), jnp.where(high_at, there, 1.0)), 0.0)
+        down = pltpu.roll(t, nx - 2 * nz, 1)
+        f = jnp.where(low_at, down * (here - there), 0.0)
+        moved = jnp.sum(f, axis=1, keepdims=True)
         weight = jnp.sum(t * lanek, axis=1, keepdims=True)
         s_rhs = s_rhs - jnp.where(edge, moved, 0.0)
         s_diag = s_diag + jnp.where(edge, weight, 0.0)
         if side:
             s_tx = s_tx + jnp.where(edge, weight, 0.0)
         edges.append(f + t)
-    border = jnp.where(even, edges[0], pltpu.roll(edges[1], nx - 1, 1))
+        spread.append(down + t)
+    border = merged(edges)
 
     for p, plane in enumerate((s_rhs, s_diag, s_ty, s_tx)):
         zplanes[iz, p] = plane
@@ -276,20 +315,24 @@
 
     def solve(z, _):
         v = poreb[z].astype(jnp.float32)
+        k01, k02 = coefficient(ktab, z, 0, 1), coefficient(ktab, z, 0, 2)
+        inv_k00 = 1.0 / rowk[pl.ds(z, 1), :]
         for side, at_row in ((0, 0), (1, ny - 1)):
             here = slice(at_row, at_row + 1)
-            for k in range(3):
-                flux[k, z, here, :] = flux[k, z, here, :] + yedge[side, pl.ds(k * nz + z, 1), :]
-            t = yedge[side, pl.ds(3 * nz + z, 1), :]
+            coarse_row, one, two, t = (yedge[side, pl.ds(k * nz + z, 1), :] for k in range(4))
+            zero_row = (coarse_row - k01 * one - k02 * two) * inv_k00
+            for k, x in enumerate((zero_row, one, two)):
+                flux[k, z, here, :] = flux[k, z, here, :] + x
             tot[z, here, :] = tot[z, here, :] + t
             at_face = HALO - 1 + side * ny
             ty[z, at_face:at_face + 1, :] = t
 
-        def beside(k):
-            shifted = pltpu.roll(border, lax.rem(2 * nx - 2 * (k * nz + z), nx), 1)
-            return jnp.where(outer, shifted, 0.0)
-
-        t = beside(3)
+        def beside(values, j):
+            return jnp.where(outer, pltpu.roll(values, lax.rem(2 * nx - 2 * j, nx), 1), 0.0)
+
+        one, two = beside(border_rest, z), beside(border_rest, nz + z)
+        added = [(beside(border, z) - k01 * one - k02 * two) * inv_k00, one, two]
+        t = beside(border, nz + z)
         txp[z] = txp[z] + jnp.where(last, t, 0.0)
         txm[z] = txm[z] + jnp.where(first, t, 0.0)
         total = tot[z] + t
@@ -302,7 +345,7 @@
                     - e[(r + 1) % 3][(c + 2) % 3] * e[(r + 2) % 3][(c + 1) % 3])
 
         cells = [u[k, z + 1, own, :] for k in range(3)]
-        f = [flux[k, z] + beside(k) for k in range(3)]
+        f = [flux[k, z] + added[k] for k in range(3)]
         res = []
         for r in range(3):
             res.append(rhs[r, z] - (v * (m[r][0] * cells[0] + m[r][1] * cells[1] + m[r][2] * cells[2])
@@ -313,9 +356,6 @@
             w[r, z] = cells[r] + (fac[0][r] * res[0] + fac[1][r] * res[1] + fac[2][r] * res[2]) * inv
             qv[r, z] = (fac[0][r] * kk[0][0] + fac[1][r] * kk[1][0] + fac[2][r] * kk[2][0]) * inv
         return 0
-
-    half = nz // 4
-    loop(0, half, solve, 0, 2)
 
     for peer in others:
         remote(zplanes.at[peer], zplanes.at[peer], z_send.at[0], z_recv.at[peer],
@@ -344,7 +384,18 @@
         coarse.append((exists(dy, dx), exists(-dy, -dx), remote(src, dst, c_send.at[s], c_recv.at[s], at(dy, dx))))
     pl.semaphore_wait(near_sem, count)
     start(coarse)
-    loop(half, nz, solve, 0, 2)
+    wait_recv(rest)
+    for side in range(2):
+        t = yedge[side, 3 * nz:, :]
+        for i in range(2):
+            part = slice(i * nz, (i + 1) * nz)
+            yedge[side, (i + 1) * nz:(i + 2) * nz, :] = t * (ysend[1, side, part, :] - yrecv[1, side, part, :])
+    edges = []
+    for side in range(2):
+        here, there = columns(1, side)
+        edges.append(jnp.where(lane < 4 * nz, spread[side] * (here - there), 0.0))
+    border_rest = merged(edges)
+    loop(0, nz, solve, 0, 2)
     wait_recv(coarse)
 
     rows = ny + 2 * HALO
@@ -389,7 +440,7 @@
     final[0] = c[0]
     final[1] = e[0]
     final[2] = ws[0]
-    wait_send(halos)
+    wait_send(halos + rest)
     for copy in sums:
         copy.wait_send()
     wait_send(coarse)
@@ -430,6 +481,7 @@
     hbm = pl.BlockSpec(memory_space=pltpu.HBM)
     dma = lambda n: pltpu.SemaphoreType.DMA((n,))
     ey = ny + 2 * HALO
+    split = upper_rows(ny)
     facets = storage_table.shape[0]
     in_vmem = pl.BlockSpec(memory_space=pltpu.VMEM)
     handed = 4 * nx * (9 * nz * ny + nz * ey + 3 * ey)
@@ -443,13 +495,13 @@
         scratch_shapes=[
             vmem(4, nz + 2, ey, nx), vmem(3, *cells),
             pltpu.VMEM(cells, permeability.dtype), pltpu.VMEM(cells, pore_volume.dtype),
-            vmem(2, 4 * nz, nx), vmem(2, 4 * nz, nx), vmem(ny, nx), vmem(2, ny, nx),
-            vmem(2, 4, ny, nx), vmem(2, 4 * nz, nx), vmem(4 * nz, nx),
+            vmem(2, 2, 2 * nz, nx), vmem(2, 2, 2 * nz, nx), vmem(2, split, nx), vmem(2, 2, split, nx),
+            vmem(2, 4, ny, nx), vmem(2, 4 * nz, nx), vmem(nz, nx),
             vmem(3, *cells), vmem(*cells),
             vmem(ngz, PLANES, ny, nx), vmem(PLANES, ey, nx),
             vmem(ny, nx), vmem(2, ey, nx), vmem(2, ey + 2 * HALO, nx),
             pltpu.SMEM((nz,), facies.dtype), pltpu.SMEM((3, facets, 3), f32), pltpu.SMEM((3, facets, 3), f32),
-            pltpu.SemaphoreType.REGULAR, dma(7), dma(6), dma(6), dma(max(ngz - 1, 1)), dma(ngz), dma(8), dma(8),
+            pltpu.SemaphoreType.REGULAR, dma(7), dma(10), dma(10), dma(max(ngz - 1, 1)), dma(ngz), dma(8), dma(8),
         ],
         compiler_params=pltpu.CompilerParams(collective_id=0, has_side_effects=True, vmem_limit_bytes=limit),
         name="cpr_apply",

time: 16.2 us -> 15.2 us (0.938)
  Pallas kernels: 15.4 us -> 14.4 us
    pallas_call x1, Pallas kernels: 13.7 us -> 12.8 us  [per_device(): pl.pallas_call(functools.partial(kernel, sizes), out_shape=(vmem(3, *cell...]
where the time goes in v5:
time: 15.2 us; the launch traced here: 15.1 us
  Pallas kernels  14.4 us (95%)
  between operations  0.64 us (4%)
    pallas_call x1, Pallas kernels, per_device(): pl.pallas_call(functools.partial(kernel, sizes), out_shape=(vmem(3, *cell...  12.8 us
    pallas_call x1, Pallas kernels, per_device(): pl.pallas_call(functools.partial(finish_kernel, parts), out_shape=(jax.Sh...  1.65 us

profile of v5, /device:TPU:0, one launch (start us, length us, event | category | flops | bytes accessed | tf_op | source)
XLA Modules:
  0.0 15.1 jit_solution(17022158456146098881)
XLA Ops:
  0.6 12.8 %cpr_apply.1 = (f32[3,16,40,128]{3,2,1,0:T(8,128)S(1)}, f32[3,16,40,128]{3,2,1,0:T(8,128)S(1)}, f32[16,40,128]{2,1,0:T(8,128)S(1)}, f32[16,56,128]{2,1,0:T(8,128...) custom-call(s32[16]{0:T(128)} %facies_hbm.1, f32[3,4,3]{2,1,0:T(4,128)} %bitcast.2, ...), custom_call_target="tpu_custom_call" | custom-call | tf_op jit(solution)/shard_map/cpr_apply/pallas_call | solution.py:489
  13.4 1.6 %cpr_finish.1 = (f32[3,16,40,128]{3,2,1,0:T(8,128)}, f32[40,128]{1,0:T(8,128)}) custom-call(f32[3,16,40,128]{3,2,1,0:T(8,128)S(1)} %get-tuple-element.9.w, f32[3,16,40,128]{3,2,1,0:T(8,128)S(1)} %get-tuple-element.10.qv, f32[16,40,128]{2,1,0:T(8,128)S(1)} %get-tuple-element.11.tzs, f32[16,56,128]{2,1,0:T(8,128)S(1)} %get-tuple-element.12.ty, ...), custom_call_target="tpu_custom_call" | custom-call | tf_op jit(solution)/shard_map/cpr_finish/pallas_call | solution.py:511

commit v6 on v5

--- a/solution.py
+++ b/solution.py
@@ -27,7 +27,7 @@
 def kernel(sizes, facies_hbm, mtab_hbm, ktab_hbm, state_hbm, rhs_hbm, perm_hbm, pore_hbm,
            w, qv, tzs, ty, txp, txm, final,
            u, rhs, permb, poreb, ysend, yrecv, xsend, xrecv, zrecv, yedge, rowk,
-           flux, tot, zplanes, ext, cxsend, cxrecv, field,
+           flux, tot, zplanes, ext, cxsend, cxrecv, cdrecv, field,
            facies, mtab, ktab, near_sem, in_sem, h_send, h_recv, z_send, z_recv, c_send, c_recv):
     ngx, ngy, ngz, nz, ny, nx = sizes
     ix, iy, iz = lax.axis_index("gx"), lax.axis_index("gy"), lax.axis_index("gz")
@@ -76,12 +76,12 @@
         (iz == ngz - 1, [zrecv.at[1]]),
         (iy == 0, [yrecv.at[:, 0], ext.at[:, 0:HALO]]),
         (iy == ngy - 1, [yrecv.at[:, 1], ext.at[:, HALO + ny:]]),
-        (ix == 0, [xrecv.at[:, 0], cxrecv.at[0, own]]),
-        (ix == ngx - 1, [xrecv.at[:, 1], cxrecv.at[1, own]]),
-        (jnp.logical_or(iy == 0, ix == 0), [cxrecv.at[0, 0:HALO]]),
-        (jnp.logical_or(iy == 0, ix == ngx - 1), [cxrecv.at[1, 0:HALO]]),
-        (jnp.logical_or(iy == ngy - 1, ix == 0), [cxrecv.at[0, HALO + ny:]]),
-        (jnp.logical_or(iy == ngy - 1, ix == ngx - 1), [cxrecv.at[1, HALO + ny:]]),
+        (ix == 0, [xrecv.at[:, 0], cxrecv.at[0]]),
+        (ix == ngx - 1, [xrecv.at[:, 1], cxrecv.at[1]]),
+        (jnp.logical_or(iy == 0, ix == 0), [cdrecv.at[0, 0]]),
+        (jnp.logical_or(iy == 0, ix == ngx - 1), [cdrecv.at[0, 1]]),
+        (jnp.logical_or(iy == ngy - 1, ix == 0), [cdrecv.at[1, 0]]),
+        (jnp.logical_or(iy == ngy - 1, ix == ngx - 1), [cdrecv.at[1, 1]]),
     ):
         @pl.when(cond)
         def _(refs=refs):
@@ -360,14 +360,24 @@
     for peer in others:
         remote(zplanes.at[peer], zplanes.at[peer], z_send.at[0], z_recv.at[peer],
                {"gx": ix, "gy": iy, "gz": peer}).wait_recv()
-    packed = nil
+    slots = nx // (PLANES * HALO)
+    groups = ny // HALO
+    tiles = cxsend.shape[1]
+    lane_group = lax.shift_right_logical(lane[:HALO], 3)
+    packed = [[nil[:HALO]] * tiles for _ in range(2)]
     for p in range(PLANES):
         plane = zplanes[0, p]
         for i in range(1, ngz):
             plane = plane + zplanes[i, p]
         ext[p, own, :] = plane
-        packed = jnp.where(lax.shift_right_logical(lane, 4) == p, pltpu.roll(plane, 2 * HALO * p + HALO, 1), packed)
-    cxsend[...] = packed
+        for g in range(groups):
+            slot = (g % slots) * PLANES + p
+            for side, shift in ((0, slot * HALO), (1, (slot + 1) * HALO)):
+                moved = pltpu.roll(plane[g * HALO:(g + 1) * HALO], shift % nx, 1)
+                packed[side][g // slots] = jnp.where(lane_group == slot, moved, packed[side][g // slots])
+    for side in range(2):
+        for tile in range(tiles):
+            cxsend[side, tile] = packed[side][tile]
 
     low, high = slice(0, HALO), slice(ny - HALO, ny)
     elow, ehigh = slice(0, HALO), slice(HALO + ny, 2 * HALO + ny)
@@ -378,9 +388,10 @@
         if dx == 0:
             src, dst = ext.at[:, slice(rows.start + HALO, rows.stop + HALO)], ext.at[:, into]
         elif dy == 0:
-            src, dst = cxsend, cxrecv.at[0 if dx > 0 else 1, own]
+            src, dst = cxsend.at[(dx + 1) // 2], cxrecv.at[(1 - dx) // 2]
         else:
-            src, dst = cxsend.at[rows], cxrecv.at[0 if dx > 0 else 1, into]
+            tile = 0 if dy < 0 else (groups - 1) // slots
+            src, dst = cxsend.at[(dx + 1) // 2, tile], cdrecv.at[(1 - dy) // 2, (1 - dx) // 2]
         coarse.append((exists(dy, dx), exists(-dy, -dx), remote(src, dst, c_send.at[s], c_recv.at[s], at(dy, dx))))
     pl.semaphore_wait(near_sem, count)
     start(coarse)
@@ -401,10 +412,21 @@
     rows = ny + 2 * HALO
     elane = lax.broadcasted_iota(jnp.int32, (rows, nx), 1)
     efirst, elast = elane == 0, elane == nx - 1
-    near = jnp.logical_or(elane < HALO, elane >= nx - HALO)
-    beside = jnp.where(lax.rem(elane, 2 * HALO) < HALO, cxrecv[0], cxrecv[1])
     a = [ext[p] for p in range(PLANES)]
-    b = [jnp.where(near, pltpu.roll(beside, nx - (2 * HALO * p + HALO), 1), 0.0) for p in range(PLANES)]
+    on_right, on_left = lane[:HALO] < HALO, lane[:HALO] >= nx - HALO
+
+    def border_of(p, g):
+        source = g % groups
+        slot = (source % slots) * PLANES + p
+        if 0 <= g < groups:
+            from_left, from_right = cxrecv[0, g // slots], cxrecv[1, g // slots]
+        else:
+            from_left, from_right = cdrecv[0 if g < 0 else 1, 0], cdrecv[0 if g < 0 else 1, 1]
+        back = (nx - slot * HALO) % nx
+        return jnp.where(on_right, pltpu.roll(from_right, back, 1),
+                         jnp.where(on_left, pltpu.roll(from_left, (back + nx - HALO) % nx, 1), 0.0))
+
+    b = [jnp.concatenate([border_of(p, g) for g in range(-1, groups + 1)], axis=0) for p in range(PLANES)]
 
     def east(a, b):
         ra, rb = pltpu.roll(a, nx - 1, 1), pltpu.roll(b, nx - 1, 1)
@@ -482,6 +504,7 @@
     dma = lambda n: pltpu.SemaphoreType.DMA((n,))
     ey = ny + 2 * HALO
     split = upper_rows(ny)
+    tiles = -(-(ny // HALO) // (nx // (PLANES * HALO)))
     facets = storage_table.shape[0]
     in_vmem = pl.BlockSpec(memory_space=pltpu.VMEM)
     handed = 4 * nx * (9 * nz * ny + nz * ey + 3 * ey)
@@ -499,7 +522,7 @@
             vmem(2, 4, ny, nx), vmem(2, 4 * nz, nx), vmem(nz, nx),
             vmem(3, *cells), vmem(*cells),
             vmem(ngz, PLANES, ny, nx), vmem(PLANES, ey, nx),
-            vmem(ny, nx), vmem(2, ey, nx), vmem(2, ey + 2 * HALO, nx),
+            vmem(2, tiles, HALO, nx), vmem(2, tiles, HALO, nx), vmem(2, 2, HALO, nx), vmem(2, ey + 2 * HALO, nx),
             pltpu.SMEM((nz,), facies.dtype), pltpu.SMEM((3, facets, 3), f32), pltpu.SMEM((3, facets, 3), f32),
             pltpu.SemaphoreType.REGULAR, dma(7), dma(10), dma(10), dma(max(ngz - 1, 1)), dma(ngz), dma(8), dma(8),
         ],

time: 15.2 us -> 15.2 us (level)
  no operation moved by 1% of the time
where the time goes in v6:
time: 15.2 us; the launch traced here: 15.1 us
  Pallas kernels  14.5 us (95%)
  between operations  0.64 us (4%)
    pallas_call x1, Pallas kernels, per_device(): pl.pallas_call(functools.partial(kernel, sizes), out_shape=(vmem(3, *cell...  12.8 us
    pallas_call x1, Pallas kernels, per_device(): pl.pallas_call(functools.partial(finish_kernel, parts), out_shape=(jax.Sh...  1.65 us

profile of v6, /device:TPU:0, one launch (start us, length us, event | category | flops | bytes accessed | tf_op | source)
XLA Modules:
  0.0 15.1 jit_solution(4451751492550790097)
XLA Ops:
  0.6 12.8 %cpr_apply.1 = (f32[3,16,40,128]{3,2,1,0:T(8,128)S(1)}, f32[3,16,40,128]{3,2,1,0:T(8,128)S(1)}, f32[16,40,128]{2,1,0:T(8,128)S(1)}, f32[16,56,128]{2,1,0:T(8,128...) custom-call(s32[16]{0:T(128)} %facies_hbm.1, f32[3,4,3]{2,1,0:T(4,128)} %bitcast.2, ...), custom_call_target="tpu_custom_call" | custom-call | tf_op jit(solution)/shard_map/cpr_apply/pallas_call | solution.py:512
  13.5 1.6 %cpr_finish.1 = (f32[3,16,40,128]{3,2,1,0:T(8,128)}, f32[40,128]{1,0:T(8,128)}) custom-call(f32[3,16,40,128]{3,2,1,0:T(8,128)S(1)} %get-tuple-element.9.w, f32[3,16,40,128]{3,2,1,0:T(8,128)S(1)} %get-tuple-element.10.qv, f32[16,40,128]{2,1,0:T(8,128)S(1)} %get-tuple-element.11.tzs, f32[16,56,128]{2,1,0:T(8,128)S(1)} %get-tuple-element.12.ty, ...), custom_call_target="tpu_custom_call" | custom-call | tf_op jit(solution)/shard_map/cpr_finish/pallas_call | solution.py:534

commit v7 on v6

--- a/solution.py
+++ b/solution.py
@@ -27,8 +27,8 @@
 def kernel(sizes, facies_hbm, mtab_hbm, ktab_hbm, state_hbm, rhs_hbm, perm_hbm, pore_hbm,
            w, qv, tzs, ty, txp, txm, final,
            u, rhs, permb, poreb, ysend, yrecv, xsend, xrecv, zrecv, yedge, rowk,
-           flux, tot, zplanes, ext, cxsend, cxrecv, cdrecv, field,
-           facies, mtab, ktab, near_sem, in_sem, h_send, h_recv, z_send, z_recv, c_send, c_recv):
+           flux, tot, zplanes, ext, cxsend, cxrecv, cdsend, cdrecv, field,
+           facies, mtab, ktab, near_sem, far_sem, in_sem, h_send, h_recv, z_send, z_recv, c_send, c_recv, d_send, d_recv):
     ngx, ngy, ngz, nz, ny, nx = sizes
     ix, iy, iz = lax.axis_index("gx"), lax.axis_index("gy"), lax.axis_index("gz")
     own = slice(HALO, HALO + ny)
@@ -50,9 +50,13 @@
         @pl.when(exists(*side))
         def _(side=side):
             pl.semaphore_signal(barrier, inc=1, device_id=at(*side), device_id_type=MESH)
-    for d in range(1, ngz):
-        pl.semaphore_signal(barrier, inc=1, device_id={"gx": ix, "gy": iy, "gz": lax.rem(iz + d, ngz)},
-                            device_id_type=MESH)
+
+    def signal_peers(sem):
+        for d in range(1, ngz):
+            pl.semaphore_signal(sem, inc=1, device_id={"gx": ix, "gy": iy, "gz": lax.rem(iz + d, ngz)},
+                                device_id_type=MESH)
+
+    signal_peers(barrier)
 
     loads = [
         pltpu.make_async_copy(perm_hbm, permb, in_sem.at[0]),
@@ -78,10 +82,10 @@
         (iy == ngy - 1, [yrecv.at[:, 1], ext.at[:, HALO + ny:]]),
         (ix == 0, [xrecv.at[:, 0], cxrecv.at[0]]),
         (ix == ngx - 1, [xrecv.at[:, 1], cxrecv.at[1]]),
-        (jnp.logical_or(iy == 0, ix == 0), [cdrecv.at[0, 0]]),
-        (jnp.logical_or(iy == 0, ix == ngx - 1), [cdrecv.at[0, 1]]),
-        (jnp.logical_or(iy == ngy - 1, ix == 0), [cdrecv.at[1, 0]]),
-        (jnp.logical_or(iy == ngy - 1, ix == ngx - 1), [cdrecv.at[1, 1]]),
+        (jnp.logical_or(iy == 0, ix == 0), [cdrecv.at[:, 0, 0]]),
+        (jnp.logical_or(iy == 0, ix == ngx - 1), [cdrecv.at[:, 0, 1]]),
+        (jnp.logical_or(iy == ngy - 1, ix == 0), [cdrecv.at[:, 1, 0]]),
+        (jnp.logical_or(iy == ngy - 1, ix == ngx - 1), [cdrecv.at[:, 1, 1]]),
     ):
         @pl.when(cond)
         def _(refs=refs):
@@ -138,6 +142,7 @@
         @pl.when(exists(*side))
         def _(side=side):
             pl.semaphore_signal(near_sem, inc=1, device_id=at(*side), device_id_type=MESH)
+    signal_peers(near_sem)
 
     def remote(src, dst, send, recv, device):
         return pltpu.make_async_remote_copy(src_ref=src, dst_ref=dst, send_sem=send, recv_sem=recv,
@@ -248,6 +253,8 @@
                 s_ty + k00 * typ, s_tx + k00 * xp)
 
     _, s_rhs, s_diag, s_ty, s_tx = loop(0, nz, assemble, (nil,) * 5, 2)
+    pl.semaphore_wait(near_sem, count + (ngz - 1))
+    signal_peers(far_sem)
     wait_recv(halos)
 
     for side, z in ((0, 0), (1, nz - 1)):
@@ -305,6 +312,29 @@
     for p, plane in enumerate((s_rhs, s_diag, s_ty, s_tx)):
         zplanes[iz, p] = plane
 
+    slots = nx // (PLANES * HALO)
+    groups = ny // HALO
+    lane_group = lax.shift_right_logical(lane[:HALO], 3)
+    for v, g in ((0, 0), (1, groups - 1)):
+        packed = [nil[:HALO]] * 2
+        for p, plane in enumerate((s_rhs, s_diag, s_ty, s_tx)):
+            for side, shift in ((0, p * HALO), (1, (p + 1) * HALO)):
+                packed[side] = jnp.where(lane_group == p, pltpu.roll(plane[g * HALO:(g + 1) * HALO], shift % nx, 1),
+                                         packed[side])
+        for side in range(2):
+            cdsend[v, side] = packed[side]
+    pl.semaphore_wait(far_sem, ngz - 1)
+    corners, arrivals = [], []
+    for n, (dy, dx) in enumerate(SIDES[4:]):
+        src, into = cdsend.at[(dy + 1) // 2, (dx + 1) // 2], ((1 - dy) // 2, (1 - dx) // 2)
+        for d in range(ngz):
+            device = {"gx": ix + dx, "gy": iy + dy, "gz": lax.rem(iz + d, ngz)}
+            corners.append((exists(dy, dx), None,
+                            remote(src, cdrecv.at[iz, into[0], into[1]], d_send.at[n * ngz + d], d_recv.at[n * ngz + iz], device)))
+            arrivals.append((None, exists(-dy, -dx),
+                             remote(src, cdrecv.at[d, into[0], into[1]], d_send.at[n * ngz + d], d_recv.at[n * ngz + d], device)))
+    start(corners)
+
     others = [lax.rem(iz + d, ngz) for d in range(1, ngz)]
     sums = [remote(zplanes.at[iz], zplanes.at[iz], z_send.at[d], z_recv.at[iz], {"gx": ix, "gy": iy, "gz": peer})
             for d, peer in enumerate(others)]
@@ -360,10 +390,7 @@
     for peer in others:
         remote(zplanes.at[peer], zplanes.at[peer], z_send.at[0], z_recv.at[peer],
                {"gx": ix, "gy": iy, "gz": peer}).wait_recv()
-    slots = nx // (PLANES * HALO)
-    groups = ny // HALO
     tiles = cxsend.shape[1]
-    lane_group = lax.shift_right_logical(lane[:HALO], 3)
     packed = [[nil[:HALO]] * tiles for _ in range(2)]
     for p in range(PLANES):
         plane = zplanes[0, p]
@@ -382,18 +409,14 @@
     low, high = slice(0, HALO), slice(ny - HALO, ny)
     elow, ehigh = slice(0, HALO), slice(HALO + ny, 2 * HALO + ny)
     coarse = []
-    for s, (dy, dx) in enumerate(SIDES):
+    for s, (dy, dx) in enumerate(SIDES[:4]):
         rows = low if dy < 0 else high
         into = ehigh if dy < 0 else elow
         if dx == 0:
             src, dst = ext.at[:, slice(rows.start + HALO, rows.stop + HALO)], ext.at[:, into]
-        elif dy == 0:
+        else:
             src, dst = cxsend.at[(dx + 1) // 2], cxrecv.at[(1 - dx) // 2]
-        else:
-            tile = 0 if dy < 0 else (groups - 1) // slots
-            src, dst = cxsend.at[(dx + 1) // 2, tile], cdrecv.at[(1 - dy) // 2, (1 - dx) // 2]
         coarse.append((exists(dy, dx), exists(-dy, -dx), remote(src, dst, c_send.at[s], c_recv.at[s], at(dy, dx))))
-    pl.semaphore_wait(near_sem, count)
     start(coarse)
     wait_recv(rest)
     for side in range(2):
@@ -408,6 +431,7 @@
     border_rest = merged(edges)
     loop(0, nz, solve, 0, 2)
     wait_recv(coarse)
+    wait_recv(arrivals)
 
     rows = ny + 2 * HALO
     elane = lax.broadcasted_iota(jnp.int32, (rows, nx), 1)
@@ -415,13 +439,17 @@
     a = [ext[p] for p in range(PLANES)]
     on_right, on_left = lane[:HALO] < HALO, lane[:HALO] >= nx - HALO
 
+    corner = [[cdrecv[0, v, side] for side in range(2)] for v in range(2)]
+    for i in range(1, ngz):
+        corner = [[corner[v][side] + cdrecv[i, v, side] for side in range(2)] for v in range(2)]
+
     def border_of(p, g):
-        source = g % groups
-        slot = (source % slots) * PLANES + p
         if 0 <= g < groups:
+            slot = (g % slots) * PLANES + p
             from_left, from_right = cxrecv[0, g // slots], cxrecv[1, g // slots]
         else:
-            from_left, from_right = cdrecv[0 if g < 0 else 1, 0], cdrecv[0 if g < 0 else 1, 1]
+            slot = p
+            from_left, from_right = corner[0 if g < 0 else 1]
         back = (nx - slot * HALO) % nx
         return jnp.where(on_right, pltpu.roll(from_right, back, 1),
                          jnp.where(on_left, pltpu.roll(from_left, (back + nx - HALO) % nx, 1), 0.0))
@@ -466,6 +494,7 @@
     for copy in sums:
         copy.wait_send()
     wait_send(coarse)
+    wait_send(corners)
 
 
 def finish_kernel(parts, w, qv, tzs, ty, txp, txm, final, new_hbm, corr_ref, out, out_sem):
@@ -522,9 +551,9 @@
             vmem(2, 4, ny, nx), vmem(2, 4 * nz, nx), vmem(nz, nx),
             vmem(3, *cells), vmem(*cells),
             vmem(ngz, PLANES, ny, nx), vmem(PLANES, ey, nx),
-            vmem(2, tiles, HALO, nx), vmem(2, tiles, HALO, nx), vmem(2, 2, HALO, nx), vmem(2, ey + 2 * HALO, nx),
+            vmem(2, tiles, HALO, nx), vmem(2, tiles, HALO, nx), vmem(2, 2, HALO, nx), vmem(ngz, 2, 2, HALO, nx), vmem(2, ey + 2 * HALO, nx),
             pltpu.SMEM((nz,), facies.dtype), pltpu.SMEM((3, facets, 3), f32), pltpu.SMEM((3, facets, 3), f32),
-            pltpu.SemaphoreType.REGULAR, dma(7), dma(10), dma(10), dma(max(ngz - 1, 1)), dma(ngz), dma(8), dma(8),
+            pltpu.SemaphoreType.REGULAR, pltpu.SemaphoreType.REGULAR, dma(7), dma(10), dma(10), dma(max(ngz - 1, 1)), dma(ngz), dma(4), dma(4), dma(4 * ngz), dma(4 * ngz),
         ],
         compiler_params=pltpu.CompilerParams(collective_id=0, has_side_effects=True, vmem_limit_bytes=limit),
         name="cpr_apply",

time: 15.2 us -> 15.1 us (level)
  Pallas kernels: 14.5 us -> 14.3 us
where the time goes in v7:
time: 15.1 us; the launch traced here: 15 us
  Pallas kernels  14.3 us (95%)
  between operations  0.64 us (4%)
    pallas_call x1, Pallas kernels, per_device(): pl.pallas_call(functools.partial(kernel, sizes), out_shape=(vmem(3, *cell...  12.7 us
    pallas_call x1, Pallas kernels, per_device(): pl.pallas_call(functools.partial(finish_kernel, parts), out_shape=(jax.Sh...  1.65 us

profile of v7, /device:TPU:0, one launch (start us, length us, event | category | flops | bytes accessed | tf_op | source)
XLA Modules:
  0.0 15.0 jit_solution(3051987052277326555)
XLA Ops:
  0.6 12.7 %cpr_apply.1 = (f32[3,16,40,128]{3,2,1,0:T(8,128)S(1)}, f32[3,16,40,128]{3,2,1,0:T(8,128)S(1)}, f32[16,40,128]{2,1,0:T(8,128)S(1)}, f32[16,56,128]{2,1,0:T(8,128...) custom-call(s32[16]{0:T(128)} %facies_hbm.1, f32[3,4,3]{2,1,0:T(4,128)} %bitcast.2, ...), custom_call_target="tpu_custom_call" | custom-call | tf_op jit(solution)/shard_map/cpr_apply/pallas_call | solution.py:541
  13.3 1.6 %cpr_finish.1 = (f32[3,16,40,128]{3,2,1,0:T(8,128)}, f32[40,128]{1,0:T(8,128)}) custom-call(f32[3,16,40,128]{3,2,1,0:T(8,128)S(1)} %get-tuple-element.9.w, f32[3,16,40,128]{3,2,1,0:T(8,128)S(1)} %get-tuple-element.10.qv, f32[16,40,128]{2,1,0:T(8,128)S(1)} %get-tuple-element.11.tzs, f32[16,56,128]{2,1,0:T(8,128)S(1)} %get-tuple-element.12.ty, ...), custom_call_target="tpu_custom_call" | custom-call | tf_op jit(solution)/shard_map/cpr_finish/pallas_call | solution.py:563
